TPU v7x, 32 devices: a whole 2x2x4 slice. The times are simulated.
32 devices in a mesh: survey: 2 (over x), freq: 16 (over z, y, core).
Axes of the slice: x: 2, y: 2, z: 4, core: 2. Of those that a mesh axis runs over, the one named last changes fastest.
Arguments:
- source: float32 [32, 2, 512, 512], P(('survey', 'freq')), parts along dimension 0, may hold values from -6 to 6
- receiver: float32 [32, 2, 512, 512], P(('survey', 'freq')), parts along dimension 0, may hold values from -6 to 6
- velocity: float32 [8, 512, 512], P('survey', 'freq'), parts along dimension 0, may hold values from 1.5 to 4.5
- anisotropy: float32 [8, 512, 512], P('survey', 'freq'), parts along dimension 0, may hold values from 0 to 0.3
- frequency: float32 [2], replicated, may hold values from 60 to 250
Outputs:
- image: float32 [8, 512, 512], P('survey', 'freq'), parts along dimension 0
There are 2 independent parts, one for each index of `survey`. A program takes and returns all parts, laid end to end along the dimension named above; an argument that names none is the same for every part. Nothing has to cross between parts.
All inputs are finite; a program needn't handle non-finite values.
Results may differ from a plain program's by a relative error of at most 0.000029.
Values sent between devices are 32-bit elements; how exact they have to be, the bound alone decides.
No kernel may reach another device: no remote copies, remote signals or barrier semaphores. Data moves between devices by JAX's collectives and lax.ppermute only.
A program may use at most 128 MiB of HBM per device.

v0:
```python
import math
import numpy as np
import jax
import jax.numpy as jnp
from jax import lax
from jax.experimental import pallas as pl
from jax.experimental.pallas import tpu as pltpu
from jax.sharding import PartitionSpec as P


LANES = 128
SUB = 8
U1 = SUB
VLIM = 28 << 20
TOP = 1.7


def even_fit(fun, degree):
    top = TOP * TOP
    nodes = 0.5 * top * (1.0 + np.cos(np.pi * (np.arange(degree + 1) + 0.5) / (degree + 1)))
    return [float(c) for c in np.polynomial.polynomial.polyfit(nodes, fun(np.sqrt(nodes)), degree)]


SIN_C = even_fit(lambda x: np.sin(x) / x, 4)
COS_C = even_fit(np.cos, 5)


def horner(coefs, z):
    acc = z * coefs[-1] + coefs[-2]
    for c in coefs[-3::-1]:
        acc = acc * z + c
    return acc


def off_of(k):
    return ((k & 3) << 1) | (k >> 2)


def at_off(o):
    return ((o & 1) << 2) | (o >> 1)


def cut(b):
    return slice(b * LANES, (b + 1) * LANES)


def iotas():
    return (lax.broadcasted_iota(jnp.int32, (SUB, LANES), 0), lax.broadcasted_iota(jnp.int32, (SUB, LANES), 1))


def pick(parts, which, index):
    out = jnp.take_along_axis(parts[0], index, axis=1)
    for a in range(1, len(parts)):
        out = jnp.where(which == a, jnp.take_along_axis(parts[a], index, axis=1), out)
    return out


def spread(parts):
    nb, lane = len(parts), iotas()[1]
    w = LANES // nb
    place = lane // w
    sorted_parts = [
        jnp.take_along_axis(x, (lane % w) * nb + (place + (nb - a)) % nb, axis=1) for a, x in enumerate(parts)
    ]
    out = []
    for b in range(nb):
        mixed = sorted_parts[0]
        for a in range(1, nb):
            mixed = jnp.where(place == (a + b) % nb, sorted_parts[a], mixed)
        out.append(pltpu.roll(mixed, LANES - w * b, 1) if b else mixed)
    return out


def turn(v):
    sub = iotas()[0]
    v = list(v)
    step = SUB // 2
    while step:
        low = (sub & step) == 0
        for a in range(SUB):
            if a & step == 0:
                x, y = v[a], v[a + step]
                v[a] = jnp.where(low, x, pltpu.roll(y, step, 0))
                v[a + step] = jnp.where(low, pltpu.roll(x, SUB - step, 0), y)
        step //= 2
    return v


def gather_back(parts):
    nb, lane = len(parts), iotas()[1]
    return [pick(parts, lane % nb, lane // nb + a * (LANES // nb)) for a in range(nb)]


def spaces():
    return [pl.BlockSpec(memory_space=s) for s in (pltpu.SMEM, pltpu.VMEM, pltpu.HBM)]


def prep_models_kernel(both, *outs):
    depth, _, R, NY = both.shape
    nb = NY // LANES

    def body(j, _):
        rows = pl.ds(pl.multiple_of(j * SUB, SUB), SUB)
        for d in range(depth):
            for m in range(2):
                for b, v in enumerate(spread([both[d, m, rows, cut(b)] for b in range(nb)])):
                    outs[d][m, rows, cut(b)] = v
                    outs[depth][d, m, rows, cut(b)] = v
        return 0

    lax.fori_loop(0, R // SUB, body, 0)


def prep_models(both):
    return pl.pallas_call(
        prep_models_kernel, out_shape=[jax.ShapeDtypeStruct(x, jnp.float32) for x in [both.shape[1:]] * both.shape[0] + [both.shape]],
        name="prep_models", compiler_params=pltpu.CompilerParams(vmem_limit_bytes=4 << 20),
        cost_estimate=pl.CostEstimate(flops=1 << 24, transcendentals=0, bytes_accessed=1 << 24),
    )(both)


def prep_field_kernel(p, sign, where, field, out):
    G, NY = out.shape[1], out.shape[3]
    nb = NY // LANES
    starts = [(where[0] ^ off_of(k)) * G for k in range(SUB)]

    def body(j, _):
        for c in range(2):
            cols = []
            for b in range(nb):
                rows = [field[p, c, pl.ds(pl.multiple_of(starts[k] + j * SUB, SUB), SUB), cut(b)] for k in range(SUB)]
                cols.append(turn(rows))
            for q in range(SUB):
                new = spread([cols[b][q] for b in range(nb)])
                for b in range(nb):
                    out[c, j * SUB + q, :, cut(b)] = -new[b] if c == 1 and sign < 0 else new[b]
        return 0

    lax.fori_loop(0, G // SUB, body, 0)


def prep_field(where, field, p, sign, G):
    NY = field.shape[-1]
    shape = (2, G, SUB, NY)
    smem, vmem, _ = spaces()
    return pl.pallas_call(
        lambda *r: prep_field_kernel(p, sign, *r), out_shape=jax.ShapeDtypeStruct(shape, jnp.float32), in_specs=[smem, vmem], out_specs=vmem, name="prep_field",
        compiler_params=pltpu.CompilerParams(vmem_limit_bytes=12 << 20),
    )(where, field)


def finish_early_kernel(scale, early, out, buf, sem):
    depth, R, NY = early.shape
    nb = NY // LANES
    for d in range(depth):
        for j in range(R // SUB):
            rows = slice(j * SUB, (j + 1) * SUB)
            new = gather_back([early[d, rows, cut(b)] * scale for b in range(nb)])
            for b in range(nb):
                buf[d, rows, cut(b)] = new[b]
    copy = pltpu.make_async_copy(buf, out.at[pl.ds(0, depth)], sem)
    copy.start()
    copy.wait()


def finish_early(scale, early):
    depth, R, NY = early.shape
    _, vmem, hbm = spaces()
    return pl.pallas_call(
        lambda *r: finish_early_kernel(scale, *r),
        out_shape=jax.ShapeDtypeStruct((depth + 1, R, NY), jnp.float32), in_specs=[vmem], out_specs=hbm,
        scratch_shapes=[pltpu.VMEM((depth, R, NY), jnp.float32), pltpu.SemaphoreType.DMA(())], name="finish_early",
        compiler_params=pltpu.CompilerParams(vmem_limit_bytes=4 << 20),
    )(early)


def finish_last_kernel(scale, own, *refs):
    far, (before, out, got, buf, sem, sem_o) = refs[:-6], refs[-6:]
    R, NY = buf.shape
    nb = NY // LANES
    copies = [pltpu.make_async_copy(ref, got.at[n], sem.at[n]) for n, ref in enumerate((own, *far))]
    for c in copies:
        c.start()
    for c in copies:
        c.wait()
    for j in range(R // SUB):
        rows = slice(j * SUB, (j + 1) * SUB)
        parts = []
        for b in range(nb):
            v = got[0, rows, cut(b)]
            for n in range(1, got.shape[0]):
                v = v + got[n, rows, cut(b)]
            parts.append(v * scale)
        new = gather_back(parts)
        for b in range(nb):
            buf[rows, cut(b)] = new[b]
    last = pltpu.make_async_copy(buf, out.at[out.shape[0] - 1], sem_o)
    last.start()
    last.wait()


def finish_last(scale, parts, before):
    R, NY = parts[0].shape
    _, _, hbm = spaces()
    n = len(parts)
    return pl.pallas_call(
        lambda *r: finish_last_kernel(scale, *r), out_shape=jax.ShapeDtypeStruct(before.shape, jnp.float32),
        in_specs=[hbm] * (n + 1), out_specs=hbm, input_output_aliases={n: 0},
        scratch_shapes=[pltpu.VMEM((n, R, NY), jnp.float32), pltpu.VMEM((R, NY), jnp.float32), pltpu.SemaphoreType.DMA((n,)), pltpu.SemaphoreType.DMA(())],
        name="finish_last", compiler_params=pltpu.CompilerParams(vmem_limit_bytes=4 << 20),
    )(*parts, before)


def wave_tools(where, G, NB):
    me_g = where[0]
    kk, lane = iotas()
    left_edge, right_edge = lane == 0, lane == LANES - 1
    g = me_g ^ off_of(kk)
    up_idx, dn_idx = (at_off(me_g ^ ((g + step) & 7)) for step in (-1, 1))
    has_up, has_dn = g > 0, g < SUB - 1

    def halos(buf):
        for c in range(4):
            for b in range(NB):
                v = buf[c, G, :, cut(b)]
                buf[c, 0, :, cut(b)] = jnp.where(has_up, jnp.take_along_axis(v, up_idx, axis=0), 0.0)
                v = buf[c, 1, :, cut(b)]
                buf[c, G + 1, :, cut(b)] = jnp.where(has_dn, jnp.take_along_axis(v, dn_idx, axis=0), 0.0)

    def around(up, mid, dn):
        r = [a + b for a, b in zip(up, dn)]
        t = [m + 0.25 * a for m, a in zip(mid, r)]
        left = [jnp.where(left_edge, 0.0, pltpu.roll(t[-1], 1, 1))] + t[:-1]
        right = t[1:] + [jnp.where(right_edge, 0.0, pltpu.roll(t[0], LANES - 1, 1))]
        return [a + (b + c) for a, b, c in zip(r, left, right)]

    def sweep(src_buf, put, base, count, done=None):
        def body(j, _):
            i0 = base + j * U1
            for f in range(2):
                rows = [[[src_buf[2 * f + c, i0 + q, :, cut(b)] for b in range(NB)] for q in range(U1 + 2)] for c in range(2)]
                for q in range(U1):
                    o = [around(rows[c][q], rows[c][q + 1], rows[c][q + 2]) for c in range(2)]
                    put(f, q, i0 + q, o, [rows[c][q + 1] for c in range(2)])
            if done is not None:
                done(i0)
            return 0

        lax.fori_loop(0, count // U1, body, 0)

    return halos, sweep


def times(mod, i, b, x, y):
    br, bi = mod[0, i, :, cut(b)], mod[1, i, :, cut(b)]
    return br * x - bi * y, br * y + bi * x


def first_kernel(cfg, where, om_ref, *refs):
    metas, R = cfg["metas"], cfg["R"]
    blks, (*cur, sh, e1, mod) = refs[: len(metas)], refs[len(metas) :]
    G, NB = mod.shape[1], mod.shape[3] // LANES
    lo = where[1]
    bases = [lo * R, (1 - lo) * R][: G // R]
    places = [[None] * SUB for _ in bases]
    for ref, (k0, kb, half, first) in zip(blks, metas):
        for k in range(kb):
            places[half][k0 + k] = (ref, first + k)
    halos, sweep = wave_tools(where, G, NB)
    om = om_ref[where[2]]
    k1 = 6.0 / om
    kp = 0.01 * om

    def cell(i, b, v, eta):
        cf = (v * k1) * (1.0 + 2.0 * eta)
        d = cf * (10.0 / 3.0)
        den = 1.0 + d * d
        inv = 1.0 / (v * den)
        ph = kp * (den * inv)
        bi = (cf * (2.0 / 3.0)) * (v * inv)
        mod[0, i, :, cut(b)] = bi * d
        mod[1, i, :, cut(b)] = bi
        z = ph * ph
        sn = ph * horner(SIN_C, z)
        cs = horner(COS_C, z)
        for f in range(2):
            re, im = cur[f][0, i, :, cut(b)], cur[f][1, i, :, cut(b)]
            sh[2 * f, i + 1, :, cut(b)] = re * cs - im * sn
            sh[2 * f + 1, i + 1, :, cut(b)] = im * cs + re * sn

    for half, base in enumerate(bases):
        def stage0(j, _):
            rows = pl.ds(pl.multiple_of(j * SUB, SUB), SUB)
            for b in range(NB):
                v, eta = (turn([ref[k, m, rows, cut(b)] for ref, k in places[half]]) for m in range(2))
                for q in range(SUB):
                    cell(base + j * SUB + q, b, v[q], eta[q])
            return 0

        lax.fori_loop(0, R // SUB, stage0, 0)
    halos(sh)

    def put(f, q, i, o, mid):
        for b in range(NB):
            x, y = times(mod, i, b, o[0][b] - 5.0 * mid[0][b], o[1][b] - 5.0 * mid[1][b])
            e1[2 * f, i + 1, :, cut(b)] = x
            e1[2 * f + 1, i + 1, :, cut(b)] = y

    sweep(sh, put, 0, G)
    halos(e1)


def second_kernel(cfg, where, sh, e1, mod, *refs):
    last, R, part = cfg["last"], cfg["R"], cfg["part"]
    G, NB = mod.shape[1], mod.shape[3] // LANES
    lo = where[1]
    bases = [lo * R, (1 - lo) * R][: G // R]
    refs = list(refs)
    e2 = refs.pop(0) if part == "kept" else None
    chosen = {"sent": [1], "kept": [0], None: list(range(len(bases)))}[part]
    outs = {o_i: refs.pop(0) for o_i in chosen}
    st = None if last else (refs.pop(0), refs.pop(0))
    e2 = refs.pop(0) if e2 is None else e2
    keep = refs
    halos, sweep = wave_tools(where, G, NB)

    def put2(f, q, i, o, mid):
        for b in range(NB):
            x, y = times(mod, i, b, o[0][b], o[1][b])
            e2[2 * f, i + 1, :, cut(b)] = x
            e2[2 * f + 1, i + 1, :, cut(b)] = y

    if part != "kept":
        sweep(e1, put2, 0, G)
        halos(e2)

    def put3(f, q, i, o, mid):
        for b in range(NB):
            x, y = times(mod, i, b, o[0][b], o[1][b])
            new = []
            for c, x in enumerate((x, y)):
                total = (x + mid[c][b]) + e1[2 * f + c, i + 1, :, cut(b)]
                new.append(sh[2 * f + c, i + 1, :, cut(b)] + (total + total))
                if not last:
                    st[f][c, i, :, cut(b)] = new[c]
                elif f == 0:
                    keep[0][c, q, :, cut(b)] = new[c]
            if f == 1:
                sr, si = (keep[0][c, q, :, cut(b)] if last else st[0][c, i, :, cut(b)] for c in range(2))
                images[b][q] = sr * new[0] - si * new[1]

    images = [[None] * SUB for _ in range(NB)]
    for o_i in reversed(chosen):
        def send(i0):
            rows = pl.ds(pl.multiple_of(i0 - bases[o_i], SUB), SUB)
            for b in range(NB):
                for k, v in enumerate(turn(images[b])):
                    outs[o_i][k, rows, cut(b)] = v

        sweep(e2, put3, bases[o_i], R, send)


def first_call(where, frequency, blocks, metas, state, R):
    _, G, _, NY = state[0].shape
    smem, vmem, _ = spaces()
    pad = jax.ShapeDtypeStruct((4, G + 2, SUB, NY), jnp.float32)
    return pl.pallas_call(
        lambda *r: first_kernel(dict(metas=metas, R=R), *r), out_shape=[pad, pad, jax.ShapeDtypeStruct((2, G, SUB, NY), jnp.float32)],
        in_specs=[smem, smem] + [vmem] * (len(blocks) + 2), out_specs=[vmem] * 3, name="first_half",
        compiler_params=pltpu.CompilerParams(vmem_limit_bytes=VLIM),
    )(where, frequency, *blocks, *state)


def second_call(where, sh, e1, mod, last, R, part=None, e2=None):
    _, G, _, NY = mod.shape
    smem, vmem, _ = spaces()
    count = G // R if part is None else 1
    out_shape = [jax.ShapeDtypeStruct((SUB, R, NY), jnp.float32)] * count
    pad = (4, G + 2, SUB, NY)
    scratch = []
    if not last:
        out_shape += [jax.ShapeDtypeStruct((2, G, SUB, NY), jnp.float32)] * 2
    if part == "sent":
        out_shape.append(jax.ShapeDtypeStruct(pad, jnp.float32))
    elif part is None:
        scratch.append(pltpu.VMEM(pad, jnp.float32))
    if last:
        scratch.append(pltpu.VMEM((2, U1, SUB, NY), jnp.float32))
    ins = [sh, e1, mod] + ([e2] if part == "kept" else [])
    return pl.pallas_call(
        lambda *r: second_kernel(dict(last=last, R=R, part=part), *r), out_shape=out_shape,
        in_specs=[smem] + [vmem] * len(ins), out_specs=[vmem] * len(out_shape),
        scratch_shapes=scratch,
        compiler_params=pltpu.CompilerParams(vmem_limit_bytes=VLIM),
    )(where, *ins)


HALF = SUB // 2


def swap(x, mask):
    n = lax.axis_size("freq")
    return lax.ppermute(x, "freq", [(i, i ^ mask) for i in range(n)])


def exchange_path(source, receiver, velocity, anisotropy, frequency, scale):
    me = lax.axis_index("freq")
    depth_count, R, _ = velocity.shape
    G = R * lax.axis_size("freq") // SUB
    where = jnp.stack([me >> 1, me & 1, lax.rem(me, frequency.shape[0])]).astype(jnp.int32)
    both = jnp.stack([velocity, anisotropy], axis=1)
    *own, all_own = prep_models(both)
    state = [prep_field(where, source, 0, 1.0, G)]
    state.append(prep_field(where, receiver, 0, -1.0, G))
    all_near = swap(all_own, 2)
    shared = [all_own, all_near, swap(all_own, 1), swap(all_near, 1)]
    corners = [(0, 0), (HALF, 0), (0, 1), (HALF, 1)]
    pieces = []
    for d in range(depth_count):
        last = d == depth_count - 1
        parts = [swap(own[d], far << 2) for far in range(1, HALF)]
        mine = jnp.stack(parts)
        near = swap(mine, 2)
        blocks = shared + [mine, near, swap(mine, 1), swap(near, 1)]
        metas = [(k0, 1, half, d) for k0, half in corners] + [(k0 + 1, HALF - 1, half, 0) for k0, half in corners]
        mid = first_call(where, frequency, blocks, metas, state, R)
        if last:
            sent, e2 = second_call(where, *mid, last, R, "sent")
            (kept,) = second_call(where, *mid, last, R, "kept", e2)
        else:
            kept, sent, *state = second_call(where, *mid, last, R)
        pieces.append((kept, swap(sent, 1)))

    def upper(d):
        return pieces[d][0][HALF:] + pieces[d][1][HALF:]

    def sums_of(depths):
        uppers = [upper(d) for d in depths]
        uppers = uppers[0] if len(depths) == 1 else jnp.stack(uppers)
        near = swap(uppers, 2)
        nears = [near] if len(depths) == 1 else [near[i] for i in range(len(depths))]
        many = [[(pieces[d][0][far] + pieces[d][1][far]) + n[far] for d, n in zip(depths, nears)] for far in range(HALF)]
        parts = [x[0] if len(x) == 1 else jnp.stack(x) for x in many]
        return [parts[0]] + [swap(parts[far], far << 2) for far in range(1, HALF)]

    early = sums_of([0])
    middle = sums_of(list(range(1, depth_count - 1)))
    tail = sums_of([depth_count - 1])
    before = jnp.concatenate([sum(early[1:], early[0])[None], sum(middle[1:], middle[0])])
    before = finish_early(scale, before)
    return finish_last(scale, tail, before)


def apart(x):
    nb = x.shape[-1] // LANES
    return jnp.swapaxes(x.reshape(x.shape[:-1] + (LANES, nb)), -1, -2).reshape(x.shape)


def together(x):
    nb = x.shape[-1] // LANES
    return jnp.swapaxes(x.reshape(x.shape[:-1] + (nb, LANES)), -1, -2).reshape(x.shape)


def gather_path(source, receiver, velocity, anisotropy, frequency, scale):
    depth_count = velocity.shape[0]
    both = lax.all_gather(apart(jnp.stack([velocity, anisotropy], axis=1)), "freq", axis=2, tiled=True)
    NX, NY = both.shape[2:]
    G = NX // SUB
    places = [off_of(k) for k in range(SUB)]
    back = [places.index(g) for g in range(SUB)]
    both = both.reshape(depth_count, 2, SUB, G, NY)
    both = jnp.stack([both[:, :, g] for g in places], axis=1)
    pairs = source.shape[0]
    ids = lax.axis_index("freq") * pairs + jnp.arange(pairs, dtype=jnp.int32)
    wheres = [jnp.stack([0 * i, 0 * i, lax.rem(i, frequency.shape[0])]).astype(jnp.int32) for i in ids]
    states = [[prep_field(wheres[p], source, p, 1.0, G), prep_field(wheres[p], receiver, p, -1.0, G)] for p in range(pairs)]
    layers = []
    for d in range(depth_count):
        total = None
        for p, state in enumerate(states):
            last = d == depth_count - 1
            mid = first_call(wheres[p], frequency, [both[d]], [(0, SUB, 0, 0)], state, G)
            res = second_call(wheres[p], *mid, last, G)
            total = res[0] if total is None else total + res[0]
            states[p] = None if last else res[1:]
        whole = jnp.concatenate([total[k] for k in back], axis=0)
        layers.append(lax.psum_scatter(whole, "freq", scatter_dimension=0, tiled=True))
    return together(jnp.stack(layers)) * scale


def use_exchange(n, rows, pairs, depth):
    return n == 2 * SUB and rows % SUB == 0 and pairs == 1 and depth == 4


def on_device(source, receiver, velocity, anisotropy, frequency):
    pair_count = source.shape[0]
    n = lax.axis_size("freq")
    exchange = use_exchange(n, velocity.shape[1], pair_count, velocity.shape[0])
    path = exchange_path if exchange else gather_path
    return path(source, receiver, velocity, anisotropy, frequency, 1.0 / math.sqrt(pair_count * n))


def solution(mesh):
    in_specs = (
        P(("survey", "freq"), None, None, None),
        P(("survey", "freq"), None, None, None),
        P("survey", "freq", None),
        P("survey", "freq", None),
        P(),
    )
    out_specs = P("survey", "freq", None)
    return jax.shard_map(
        on_device, mesh=mesh, in_specs=in_specs, out_specs=out_specs, check_vma=False
    )
```

profile of v0, /device:TPU:0, one launch (start us, length us, event | category | flops | bytes accessed | tf_op | source)
XLA Modules:
  0.0 164.9 jit_solution(8629082995489277532)
XLA Ops:
  2.0 3.1 %collective-permute-start.21 = (f32[2,32,512]{2,1,0:T(8,128)S(1)}, f32[2,32,512]{2,1,0:T(8,128)S(1)}, u32[]{:S(2)}, u32[]{:S(2)}) collective-permute-start(f32[2,32,512]{2,1,0:T(8,128)S(1)} %get-tuple-element.40), channel_id=1, source_target_pairs={{0,4},{1,5},{2,6},{3,7},{4,0},{5,1},{6,2},{7,3},{8,12},{9,13},{10,... | collective-permute-start | bytes 393224 | tf_op jit(solution)/shard_map/ppermute | solution.py:403
  10.2 3.4 %collective-permute-start.16 = (f32[2,32,512]{2,1,0:T(8,128)S(1)}, f32[2,32,512]{2,1,0:T(8,128)S(1)}, u32[]{:S(2)}, u32[]{:S(2)}) collective-permute-start(f32[2,32,512]{2,1,0:T(8,128)S(1)} %get-tuple-element.39), channel_id=1, source_target_pairs={{0,8},{1,9},{2,10},{3,11},{4,12},{5,13},{6,14},{7,15},{8,0},{9,1},... | collective-permute-start | bytes 393224 | tf_op jit(solution)/shard_map/ppermute | solution.py:403
  13.6 4.4 %collective-permute-done.22 = f32[2,32,512]{2,1,0:T(8,128)S(1)} collective-permute-done((f32[2,32,512]{2,1,0:T(8,128)S(1)}, f32[2,32,512]{2,1,0:T(8,128)S(1)}, u32[]{:S(2)}, u32[]{:S(2)}) %collective-permute-start.22) | collective-permute-done | bytes 131104 | tf_op jit(solution)/shard_map/ppermute | solution.py:403
  21.8 9.4 %collective-permute-start.9 = (f32[2,32,512]{2,1,0:T(8,128)S(1)}, f32[2,32,512]{2,1,0:T(8,128)S(1)}, u32[]{:S(2)}, u32[]{:S(2)}) collective-permute-start(f32[2,32,512]{2,1,0:T(8,128)S(1)} %get-tuple-element.38), channel_id=1, source_target_pairs={{0,4},{1,5},{2,6},{3,7},{4,0},{5,1},{6,2},{7,3},{8,12},{9,13},{10,... | collective-permute-start | bytes 393224 | tf_op jit(solution)/shard_map/ppermute | solution.py:403
  36.2 3.4 %collective-permute-start.3 = (f32[2,32,512]{2,1,0:T(8,128)S(1)}, f32[2,32,512]{2,1,0:T(8,128)S(1)}, u32[]{:S(2)}, u32[]{:S(2)}) collective-permute-start(f32[2,32,512]{2,1,0:T(8,128)S(1)} %get-tuple-element.37), channel_id=1, source_target_pairs={{0,4},{1,5},{2,6},{3,7},{4,0},{5,1},{6,2},{7,3},{8,12},{9,13},{10,... | collective-permute-start | bytes 393224 | tf_op jit(solution)/shard_map/ppermute | solution.py:403
  40.5 4.2 %collective-permute-done.10 = f32[2,32,512]{2,1,0:T(8,128)S(1)} collective-permute-done((f32[2,32,512]{2,1,0:T(8,128)S(1)}, f32[2,32,512]{2,1,0:T(8,128)S(1)}, u32[]{:S(2)}, u32[]{:S(2)}) %collective-permute-start.10) | collective-permute-done | bytes 131104 | tf_op jit(solution)/shard_map/ppermute | solution.py:403
  47.5 3.2 %collective-permute-start.5 = (f32[2,32,512]{2,1,0:T(8,128)S(1)}, f32[2,32,512]{2,1,0:T(8,128)S(1)}, u32[]{:S(2)}, u32[]{:S(2)}) collective-permute-start(f32[2,32,512]{2,1,0:T(8,128)S(1)} %get-tuple-element.37), channel_id=1, source_target_pairs={{0,12},{1,13},{2,14},{3,15},{4,8},{5,9},{6,10},{7,11},{8,4},{9,5},... | collective-permute-start | bytes 393224 | tf_op jit(solution)/shard_map/ppermute | solution.py:403
  57.0 9.6 %collective-permute-done.18.r_7_ = f32[3,2,32,512]{3,2,1,0:T(8,128)} collective-permute-done((f32[3,2,32,512]{3,2,1,0:T(8,128)}, f32[3,2,32,512]{3,2,1,0:T(8,128)}, u32[]{:S(2)}, u32[]{:S(2)}) %collective-permute-start.18) | collective-permute-done | bytes 393248 | tf_op jit(solution)/shard_map/ppermute | solution.py:403
  71.0 3.5 %prep_field.2.r_10_ = f32[2,64,8,512]{3,2,1,0:T(8,128)S(1)} custom-call(s32[3]{0:T(128)S(1)} %pad_add_fusion.r_0_, f32[1,2,512,512]{3,2,1,0:T(8,128)S(1)} %copy-done), custom_call_target="tpu_custom_call" | custom-call | tf_op jit(solution)/shard_map/prep_field/pallas_call | solution.py:146
  74.6 3.5 %prep_field.3.r_11_ = f32[2,64,8,512]{3,2,1,0:T(8,128)S(1)} custom-call(s32[3]{0:T(128)S(1)} %pad_add_fusion.r_0_, f32[1,2,512,512]{3,2,1,0:T(8,128)S(1)} %copy-done.1), custom_call_target="tpu_custom_call" | custom-call | tf_op jit(solution)/shard_map/prep_field/pallas_call | solution.py:146
  78.2 4.5 %first_half.4 = (f32[4,66,8,512]{3,2,1,0:T(8,128)S(1)}, f32[4,66,8,512]{3,2,1,0:T(8,128)S(1)}, f32[2,64,8,512]{3,2,1,0:T(8,128)S(1)}) custom-call(s32[3]{0:T(128)S(1)} %pad_add_fusion.r_0_, f32[2]{0:T(128)S(1)} %copy-done.8, f32[4,2,32,512]{3,2,1,0:T(8,128)S(1)} %get-tuple-element.36.r_2_, f32[4,2,32,512]{3,2,1,0:T(8,128)S(1)} %collective-permute-done.r_3_, ...), custom_call_target="tpu_custom_call" | custom-call | tf_op jit(solution)/shard_map/first_half/pallas_call | solution.py:367
  82.7 4.4 %shard_map.55 = (f32[8,32,512]{2,1,0:T(8,128)S(1)}, f32[8,32,512]{2,1,0:T(8,128)S(1)}, f32[2,64,8,512]{3,2,1,0:T(8,128)S(1)}, f32[2,64,8,512]{3,2,1,0:T(8,128)S(1)}) custom-call(s32[3]{0:T(128)S(1)} %pad_add_fusion.r_0_, f32[4,66,8,512]{3,2,1,0:T(8,128)S(1)} %get-tuple-element.41.r_1_, f32[4,66,8,512]{3,2,1,0:T(8,128)S(1)} %get-tuple-element.42.r_2_, ...), custom_call_target="tpu_custom_call" | custom-call | tf_op jit(solution)/shard_map/pallas_call | solution.py:390
  88.3 5.3 %first_half.5 = (f32[4,66,8,512]{3,2,1,0:T(8,128)S(1)}, f32[4,66,8,512]{3,2,1,0:T(8,128)S(1)}, f32[2,64,8,512]{3,2,1,0:T(8,128)S(1)}) custom-call(s32[3]{0:T(128)S(1)} %pad_add_fusion.r_0_, f32[2]{0:T(128)S(1)} %copy-done.8, f32[4,2,32,512]{3,2,1,0:T(8,128)S(1)} %get-tuple-element.36.r_2_, f32[4,2,32,512]{3,2,1,0:T(8,128)S(1)} %collective-permute-done.r_3_, ...), custom_call_target="tpu_custom_call" | custom-call | tf_op jit(solution)/shard_map/first_half/pallas_call | solution.py:367
  93.6 4.4 %shard_map.56 = (f32[8,32,512]{2,1,0:T(8,128)S(1)}, f32[8,32,512]{2,1,0:T(8,128)S(1)}, f32[2,64,8,512]{3,2,1,0:T(8,128)S(1)}, f32[2,64,8,512]{3,2,1,0:T(8,128)S(1)}) custom-call(s32[3]{0:T(128)S(1)} %pad_add_fusion.r_0_, f32[4,66,8,512]{3,2,1,0:T(8,128)S(1)} %get-tuple-element.46.r_1_, f32[4,66,8,512]{3,2,1,0:T(8,128)S(1)} %get-tuple-element.47.r_2_, ...), custom_call_target="tpu_custom_call" | custom-call | tf_op jit(solution)/shard_map/pallas_call | solution.py:390
  98.2 5.1 %first_half.6 = (f32[4,66,8,512]{3,2,1,0:T(8,128)S(1)}, f32[4,66,8,512]{3,2,1,0:T(8,128)S(1)}, f32[2,64,8,512]{3,2,1,0:T(8,128)S(1)}) custom-call(s32[3]{0:T(128)S(1)} %pad_add_fusion.r_0_, f32[2]{0:T(128)S(1)} %copy-done.8, f32[4,2,32,512]{3,2,1,0:T(8,128)S(1)} %get-tuple-element.36.r_2_, f32[4,2,32,512]{3,2,1,0:T(8,128)S(1)} %collective-permute-done.r_3_, ...), custom_call_target="tpu_custom_call" | custom-call | tf_op jit(solution)/shard_map/first_half/pallas_call | solution.py:367
  103.3 4.4 %shard_map.57 = (f32[8,32,512]{2,1,0:T(8,128)S(1)}, f32[8,32,512]{2,1,0:T(8,128)S(1)}, f32[2,64,8,512]{3,2,1,0:T(8,128)S(1)}, f32[2,64,8,512]{3,2,1,0:T(8,128)S(1)}) custom-call(s32[3]{0:T(128)S(1)} %pad_add_fusion.r_0_, f32[4,66,8,512]{3,2,1,0:T(8,128)S(1)} %get-tuple-element.51.r_1_, f32[4,66,8,512]{3,2,1,0:T(8,128)S(1)} %get-tuple-element.52.r_2_, ...), custom_call_target="tpu_custom_call" | custom-call | tf_op jit(solution)/shard_map/pallas_call | solution.py:390
  108.3 5.0 %first_half.7 = (f32[4,66,8,512]{3,2,1,0:T(8,128)S(1)}, f32[4,66,8,512]{3,2,1,0:T(8,128)S(1)}, f32[2,64,8,512]{3,2,1,0:T(8,128)S(1)}) custom-call(s32[3]{0:T(128)S(1)} %pad_add_fusion.r_0_, f32[2]{0:T(128)S(1)} %copy-done.8, f32[4,2,32,512]{3,2,1,0:T(8,128)S(1)} %get-tuple-element.36.r_2_, f32[4,2,32,512]{3,2,1,0:T(8,128)S(1)} %collective-permute-done.r_3_, ...), custom_call_target="tpu_custom_call" | custom-call | tf_op jit(solution)/shard_map/first_half/pallas_call | solution.py:367
  113.3 3.2 %shard_map.58 = (f32[8,32,512]{2,1,0:T(8,128)S(1)}, f32[4,66,8,512]{3,2,1,0:T(8,128)S(1)}) custom-call(s32[3]{0:T(128)S(1)} %pad_add_fusion.r_0_, f32[4,66,8,512]{3,2,1,0:T(8,128)S(1)} %get-tuple-element.56.r_1_, f32[4,66,8,512]{3,2,1,0:T(8,128)S(1)} %get-tuple-element.57.r_2_, f32[2,64,8,512]{3,2,1,0:T(8,128)S(1)} %get-tuple-element.58.r_3_), custom_call_target="tpu_custom_call" | custom-call | tf_op jit(solution)/shard_map/pallas_call | solution.py:390
  121.4 6.3 %collective-permute-done.33 = f32[4,32,512]{2,1,0:T(8,128)S(1)} collective-permute-done((f32[4,32,512]{2,1,0:T(8,128)S(1)}, f32[4,32,512]{2,1,0:T(8,128)S(1)}, u32[]{:S(2)}, u32[]{:S(2)}) %collective-permute-start.33) | collective-permute-done | bytes 262176 | tf_op jit(solution)/shard_map/ppermute | solution.py:403
  127.9 3.8 %collective-permute-start.35 = (f32[32,512]{1,0:T(8,128)S(1)}, f32[32,512]{1,0:T(8,128)S(1)}, u32[]{:S(2)}, u32[]{:S(2)}) collective-permute-start(f32[32,512]{1,0:T(8,128)S(1)} %get-tuple-element.77), channel_id=1, source_target_pairs={{0,8},{1,9},{2,10},{3,11},{4,12},{5,13},{6,14},{7,15},{8,0},{9,1},... | collective-permute-start | bytes 196616 | tf_op jit(solution)/shard_map/ppermute | solution.py:403
  132.3 11.8 %collective-permute-done.28 = f32[4,32,512]{2,1,0:T(8,128)S(1)} collective-permute-done((f32[4,32,512]{2,1,0:T(8,128)S(1)}, f32[4,32,512]{2,1,0:T(8,128)S(1)}, u32[]{:S(2)}, u32[]{:S(2)}) %collective-permute-start.28) | collective-permute-done | bytes 262176 | tf_op jit(solution)/shard_map/ppermute | solution.py:403
  144.2 3.7 %collective-permute-start.30 = (f32[32,512]{1,0:T(8,128)S(1)}, f32[32,512]{1,0:T(8,128)S(1)}, u32[]{:S(2)}, u32[]{:S(2)}) collective-permute-start(f32[32,512]{1,0:T(8,128)S(1)} %get-tuple-element.79), channel_id=1, source_target_pairs={{0,8},{1,9},{2,10},{3,11},{4,12},{5,13},{6,14},{7,15},{8,0},{9,1},... | collective-permute-start | bytes 196616 | tf_op jit(solution)/shard_map/ppermute | solution.py:403
  149.4 3.2 %collective-permute-start.42 = (f32[2,32,512]{2,1,0:T(8,128)S(1)}, f32[2,32,512]{2,1,0:T(8,128)S(1)}, u32[]{:S(2)}, u32[]{:S(2)}) collective-permute-start(f32[2,32,512]{2,1,0:T(8,128)S(1)} %pad_maximum_fusion.9), channel_id=1, source_target_pairs={{0,12},{1,13},{2,14},{3,15},{4,8},{5,9},{6,10},{7,11},{8,4},{9,5},... | collective-permute-start | bytes 393224 | tf_op jit(solution)/shard_map/ppermute | solution.py:403
  158.0 4.4 %collective-permute-done.41 = f32[2,32,512]{2,1,0:T(8,128)S(1)} collective-permute-done((f32[2,32,512]{2,1,0:T(8,128)S(1)}, f32[2,32,512]{2,1,0:T(8,128)S(1)}, u32[]{:S(2)}, u32[]{:S(2)}) %collective-permute-start.41) | collective-permute-done | bytes 131104 | tf_op jit(solution)/shard_map/ppermute | solution.py:403
  (115 shorter events, 47.0 us)
Async XLA Ops:
  7.7 43.0 %collective-permute-start = (f32[4,2,32,512]{3,2,1,0:T(8,128)S(1)}, f32[4,2,32,512]{3,2,1,0:T(8,128)S(1)}, u32[]{:S(2)}, u32[]{:S(2)}) collective-permute-start(f32[4,2,32,512]{3,2,1,0:T(8,128)S(1)} %get-tuple-element.36.r_2_), channel_id=1, source_target_pairs={{0,2},{1,3},{2,0},{3,1},{4,6},{5,7},{6,4},{7,5},{8,10},{9,11},{10,... | collective-permute-start | bytes 1572872 | tf_op jit(solution)/shard_map/ppermute | solution.py:403
  10.2 21.9 %collective-permute-start.16 = (f32[2,32,512]{2,1,0:T(8,128)S(1)}, f32[2,32,512]{2,1,0:T(8,128)S(1)}, u32[]{:S(2)}, u32[]{:S(2)}) collective-permute-start(f32[2,32,512]{2,1,0:T(8,128)S(1)} %get-tuple-element.39), channel_id=1, source_target_pairs={{0,8},{1,9},{2,10},{3,11},{4,12},{5,13},{6,14},{7,15},{8,0},{9,1},... | collective-permute-start | bytes 393224 | tf_op jit(solution)/shard_map/ppermute | solution.py:403
  18.0 15.6 %collective-permute-start.17 = (f32[2,32,512]{2,1,0:T(8,128)S(1)}, f32[2,32,512]{2,1,0:T(8,128)S(1)}, u32[]{:S(2)}, u32[]{:S(2)}) collective-permute-start(f32[2,32,512]{2,1,0:T(8,128)S(1)} %get-tuple-element.39), channel_id=1, source_target_pairs={{0,12},{1,13},{2,14},{3,15},{4,8},{5,9},{6,10},{7,11},{8,4},{9,5},... | collective-permute-start | bytes 393224 | tf_op jit(solution)/shard_map/ppermute | solution.py:403
  20.9 15.3 %collective-permute-start.11 = (f32[2,32,512]{2,1,0:T(8,128)S(1)}, f32[2,32,512]{2,1,0:T(8,128)S(1)}, u32[]{:S(2)}, u32[]{:S(2)}) collective-permute-start(f32[2,32,512]{2,1,0:T(8,128)S(1)} %get-tuple-element.38), channel_id=1, source_target_pairs={{0,12},{1,13},{2,14},{3,15},{4,8},{5,9},{6,10},{7,11},{8,4},{9,5},... | collective-permute-start | bytes 393224 | tf_op jit(solution)/shard_map/ppermute | solution.py:403
  21.8 17.8 %collective-permute-start.9 = (f32[2,32,512]{2,1,0:T(8,128)S(1)}, f32[2,32,512]{2,1,0:T(8,128)S(1)}, u32[]{:S(2)}, u32[]{:S(2)}) collective-permute-start(f32[2,32,512]{2,1,0:T(8,128)S(1)} %get-tuple-element.38), channel_id=1, source_target_pairs={{0,4},{1,5},{2,6},{3,7},{4,0},{5,1},{6,2},{7,3},{8,12},{9,13},{10,... | collective-permute-start | bytes 393224 | tf_op jit(solution)/shard_map/ppermute | solution.py:403
  32.0 23.8 %collective-permute-start.24 = (f32[3,2,32,512]{3,2,1,0:T(8,128)S(1)}, f32[3,2,32,512]{3,2,1,0:T(8,128)S(1)}, u32[]{:S(2)}, u32[]{:S(2)}) collective-permute-start(f32[3,2,32,512]{3,2,1,0:T(8,128)S(1)} %pad_maximum_fusion.5.r_6_), channel_id=1, source_target_pairs={{0,2},{1,3},{2,0},{3,1},{4,6},{5,7},{6,4},{7,5},{8,10},{9,11},{10,... | collective-permute-start | bytes 1179656 | tf_op jit(solution)/shard_map/ppermute | solution.py:403
  50.7 18.1 %collective-permute-start.2 = (f32[4,2,32,512]{3,2,1,0:T(8,128)S(1)}, f32[4,2,32,512]{3,2,1,0:T(8,128)S(1)}, u32[]{:S(2)}, u32[]{:S(2)}) collective-permute-start(f32[4,2,32,512]{3,2,1,0:T(8,128)S(1)} %collective-permute-done.r_3_), channel_id=1, source_target_pairs={{0,1},{1,0},{2,3},{3,2},{4,5},{5,4},{6,7},{7,6},{8,9},{9,8},{10,11... | collective-permute-start | bytes 1572872 | tf_op jit(solution)/shard_map/ppermute | solution.py:403
  55.8 31.3 %collective-permute-start.19 = (f32[3,2,32,512]{3,2,1,0:T(8,128)}, f32[3,2,32,512]{3,2,1,0:T(8,128)}, u32[]{:S(2)}, u32[]{:S(2)}) collective-permute-start(f32[3,2,32,512]{3,2,1,0:T(8,128)} %pad_maximum_fusion.4.r_6_), channel_id=1, source_target_pairs={{0,1},{1,0},{2,3},{3,2},{4,5},{5,4},{6,7},{7,6},{8,9},{9,8},{10,11... | collective-permute-start | bytes 1179656 | tf_op jit(solution)/shard_map/ppermute | solution.py:403
  56.4 30.9 %collective-permute-start.12 = (f32[3,2,32,512]{3,2,1,0:T(8,128)S(1)}, f32[3,2,32,512]{3,2,1,0:T(8,128)}, u32[]{:S(2)}, u32[]{:S(2)}) collective-permute-start(f32[3,2,32,512]{3,2,1,0:T(8,128)S(1)} %pad_maximum_fusion.3.r_6_), channel_id=1, source_target_pairs={{0,2},{1,3},{2,0},{3,1},{4,6},{5,7},{6,4},{7,5},{8,10},{9,11},{10,... | collective-permute-start | bytes 1179656 | tf_op jit(solution)/shard_map/ppermute | solution.py:403
  66.6 21.2 %collective-permute-start.6 = (f32[3,2,32,512]{3,2,1,0:T(8,128)S(1)}, f32[3,2,32,512]{3,2,1,0:T(8,128)}, u32[]{:S(2)}, u32[]{:S(2)}) collective-permute-start(f32[3,2,32,512]{3,2,1,0:T(8,128)S(1)} %pad_maximum_fusion.2.r_6_), channel_id=1, source_target_pairs={{0,2},{1,3},{2,0},{3,1},{4,6},{5,7},{6,4},{7,5},{8,10},{9,11},{10,... | collective-permute-start | bytes 1179656 | tf_op jit(solution)/shard_map/ppermute | solution.py:403
  68.8 19.0 %collective-permute-start.20 = (f32[3,2,32,512]{3,2,1,0:T(8,128)}, f32[3,2,32,512]{3,2,1,0:T(8,128)}, u32[]{:S(2)}, u32[]{:S(2)}) collective-permute-start(f32[3,2,32,512]{3,2,1,0:T(8,128)} %collective-permute-done.18.r_7_), channel_id=1, source_target_pairs={{0,1},{1,0},{2,3},{3,2},{4,5},{5,4},{6,7},{7,6},{8,9},{9,8},{10,11... | collective-permute-start | bytes 1179656 | tf_op jit(solution)/shard_map/ppermute | solution.py:403
  68.9 29.2 %collective-permute-start.13 = (f32[3,2,32,512]{3,2,1,0:T(8,128)S(1)}, f32[3,2,32,512]{3,2,1,0:T(8,128)}, u32[]{:S(2)}, u32[]{:S(2)}) collective-permute-start(f32[3,2,32,512]{3,2,1,0:T(8,128)S(1)} %pad_maximum_fusion.3.r_6_), channel_id=1, source_target_pairs={{0,1},{1,0},{2,3},{3,2},{4,5},{5,4},{6,7},{7,6},{8,9},{9,8},{10,11... | collective-permute-start | bytes 1179656 | tf_op jit(solution)/shard_map/ppermute | solution.py:403
  87.2 31.3 %collective-permute-start.32 = (f32[8,32,512]{2,1,0:T(8,128)S(1)}, f32[8,32,512]{2,1,0:T(8,128)S(1)}, u32[]{:S(2)}, u32[]{:S(2)}) collective-permute-start(f32[8,32,512]{2,1,0:T(8,128)S(1)} %get-tuple-element.62), channel_id=1, source_target_pairs={{0,1},{1,0},{2,3},{3,2},{4,5},{5,4},{6,7},{7,6},{8,9},{9,8},{10,11... | collective-permute-start | bytes 1572872 | tf_op jit(solution)/shard_map/ppermute | solution.py:403
  87.8 20.5 %collective-permute-start.7 = (f32[3,2,32,512]{3,2,1,0:T(8,128)S(1)}, f32[3,2,32,512]{3,2,1,0:T(8,128)S(1)}, u32[]{:S(2)}, u32[]{:S(2)}) collective-permute-start(f32[3,2,32,512]{3,2,1,0:T(8,128)S(1)} %pad_maximum_fusion.2.r_6_), channel_id=1, source_target_pairs={{0,1},{1,0},{2,3},{3,2},{4,5},{5,4},{6,7},{7,6},{8,9},{9,8},{10,11... | collective-permute-start | bytes 1179656 | tf_op jit(solution)/shard_map/ppermute | solution.py:403
  87.8 20.4 %collective-permute-start.8 = (f32[3,2,32,512]{3,2,1,0:T(8,128)}, f32[3,2,32,512]{3,2,1,0:T(8,128)S(1)}, u32[]{:S(2)}, u32[]{:S(2)}) collective-permute-start(f32[3,2,32,512]{3,2,1,0:T(8,128)} %collective-permute-done.6.r_7_), channel_id=1, source_target_pairs={{0,1},{1,0},{2,3},{3,2},{4,5},{5,4},{6,7},{7,6},{8,9},{9,8},{10,11... | collective-permute-start | bytes 1179656 | tf_op jit(solution)/shard_map/ppermute | solution.py:403
  98.1 21.0 %collective-permute-start.37 = (f32[8,32,512]{2,1,0:T(8,128)S(1)}, f32[8,32,512]{2,1,0:T(8,128)S(1)}, u32[]{:S(2)}, u32[]{:S(2)}) collective-permute-start(f32[8,32,512]{2,1,0:T(8,128)S(1)} %get-tuple-element.64), channel_id=1, source_target_pairs={{0,1},{1,0},{2,3},{3,2},{4,5},{5,4},{6,7},{7,6},{8,9},{9,8},{10,11... | collective-permute-start | bytes 1572872 | tf_op jit(solution)/shard_map/ppermute | solution.py:403
  119.2 25.0 %collective-permute-start.39 = (f32[2,4,32,512]{3,2,1,0:T(8,128)S(1)}, f32[2,4,32,512]{3,2,1,0:T(8,128)S(1)}, u32[]{:S(2)}, u32[]{:S(2)}) collective-permute-start(f32[2,4,32,512]{3,2,1,0:T(8,128)S(1)} %pad_maximum_fusion.1), channel_id=1, source_target_pairs={{0,2},{1,3},{2,0},{3,1},{4,6},{5,7},{6,4},{7,5},{8,10},{9,11},{10,... | collective-permute-start | bytes 1572872 | tf_op jit(solution)/shard_map/ppermute | solution.py:403
  120.9 23.2 %collective-permute-start.28 = (f32[4,32,512]{2,1,0:T(8,128)S(1)}, f32[4,32,512]{2,1,0:T(8,128)S(1)}, u32[]{:S(2)}, u32[]{:S(2)}) collective-permute-start(f32[4,32,512]{2,1,0:T(8,128)S(1)} %slice_add_fusion.3), channel_id=1, source_target_pairs={{0,2},{1,3},{2,0},{3,1},{4,6},{5,7},{6,4},{7,5},{8,10},{9,11},{10,... | collective-permute-start | bytes 786440 | tf_op jit(solution)/shard_map/ppermute | solution.py:403
  127.8 20.4 %collective-permute-start.34 = (f32[32,512]{1,0:T(8,128)S(1)}, f32[32,512]{1,0:T(8,128)S(1)}, u32[]{:S(2)}, u32[]{:S(2)}) collective-permute-start(f32[32,512]{1,0:T(8,128)S(1)} %get-tuple-element.75), channel_id=1, source_target_pairs={{0,4},{1,5},{2,6},{3,7},{4,0},{5,1},{6,2},{7,3},{8,12},{9,13},{10,... | collective-permute-start | bytes 196616 | tf_op jit(solution)/shard_map/ppermute | solution.py:403
  127.9 20.5 %collective-permute-start.35 = (f32[32,512]{1,0:T(8,128)S(1)}, f32[32,512]{1,0:T(8,128)S(1)}, u32[]{:S(2)}, u32[]{:S(2)}) collective-permute-start(f32[32,512]{1,0:T(8,128)S(1)} %get-tuple-element.77), channel_id=1, source_target_pairs={{0,8},{1,9},{2,10},{3,11},{4,12},{5,13},{6,14},{7,15},{8,0},{9,1},... | collective-permute-start | bytes 196616 | tf_op jit(solution)/shard_map/ppermute | solution.py:403
  131.6 17.8 %collective-permute-start.36 = (f32[32,512]{1,0:T(8,128)S(1)}, f32[32,512]{1,0:T(8,128)S(1)}, u32[]{:S(2)}, u32[]{:S(2)}) collective-permute-start(f32[32,512]{1,0:T(8,128)S(1)} %get-tuple-element.76), channel_id=1, source_target_pairs={{0,12},{1,13},{2,14},{3,15},{4,8},{5,9},{6,10},{7,11},{8,4},{9,5},... | collective-permute-start | bytes 196616 | tf_op jit(solution)/shard_map/ppermute | solution.py:403
  144.1 19.5 %collective-permute-start.29 = (f32[32,512]{1,0:T(8,128)S(1)}, f32[32,512]{1,0:T(8,128)S(1)}, u32[]{:S(2)}, u32[]{:S(2)}) collective-permute-start(f32[32,512]{1,0:T(8,128)S(1)} %get-tuple-element.80), channel_id=1, source_target_pairs={{0,4},{1,5},{2,6},{3,7},{4,0},{5,1},{6,2},{7,3},{8,12},{9,13},{10,... | collective-permute-start | bytes 196616 | tf_op jit(solution)/shard_map/ppermute | solution.py:403
  144.2 19.4 %collective-permute-start.30 = (f32[32,512]{1,0:T(8,128)S(1)}, f32[32,512]{1,0:T(8,128)S(1)}, u32[]{:S(2)}, u32[]{:S(2)}) collective-permute-start(f32[32,512]{1,0:T(8,128)S(1)} %get-tuple-element.79), channel_id=1, source_target_pairs={{0,8},{1,9},{2,10},{3,11},{4,12},{5,13},{6,14},{7,15},{8,0},{9,1},... | collective-permute-start | bytes 196616 | tf_op jit(solution)/shard_map/ppermute | solution.py:403
  148.3 14.1 %collective-permute-start.41 = (f32[2,32,512]{2,1,0:T(8,128)S(1)}, f32[2,32,512]{2,1,0:T(8,128)S(1)}, u32[]{:S(2)}, u32[]{:S(2)}) collective-permute-start(f32[2,32,512]{2,1,0:T(8,128)S(1)} %pad_maximum_fusion.8), channel_id=1, source_target_pairs={{0,8},{1,9},{2,10},{3,11},{4,12},{5,13},{6,14},{7,15},{8,0},{9,1},... | collective-permute-start | bytes 393224 | tf_op jit(solution)/shard_map/ppermute | solution.py:403
  (28 other events, 225.2 us)
where the time goes:
time: 165 us
  starting transfers between devices  61.9 us (38%)
  waiting for transfers between devices  49 us (30%)
  Pallas kernels  48.6 us (29%)
  other arithmetic  2.61 us (2%)
  local copies, waits for them, and re-layouts  2.37 us (1%)
    ppermute x43, starting transfers between devices, swap(): return lax.ppermute(x, 'freq', [(i, i ^ mask) for i in range(n)])  61.9 us
    ppermute x43, waiting for transfers between devices, swap(): return lax.ppermute(x, 'freq', [(i, i ^ mask) for i in range(n)])  49 us
    pallas_call x4, Pallas kernels, first_call(): pl.pallas_call(lambda *r: first_kernel(dict(metas=metas, R=R), *r), out_s...  20 us
    pallas_call x5, Pallas kernels, second_call(): pl.pallas_call(lambda *r: second_kernel(dict(last=last, R=R, part=part),...  18.3 us
    pallas_call x2, Pallas kernels, prep_field(): pl.pallas_call(lambda *r: prep_field_kernel(p, sign, *r), out_shape=jax.S...  7.05 us
  transfers between devices with their start and end apart: 43, of which 11 were waited for; matrix products, arithmetic and copies ran while one was open for 1% of the time, Pallas kernels for 28%

commit v1 on v0

--- a/solution.py
+++ b/solution.py
@@ -434,19 +434,20 @@
     def upper(d):
         return pieces[d][0][HALF:] + pieces[d][1][HALF:]
 
-    def sums_of(depths):
-        uppers = [upper(d) for d in depths]
-        uppers = uppers[0] if len(depths) == 1 else jnp.stack(uppers)
-        near = swap(uppers, 2)
-        nears = [near] if len(depths) == 1 else [near[i] for i in range(len(depths))]
-        many = [[(pieces[d][0][far] + pieces[d][1][far]) + n[far] for d, n in zip(depths, nears)] for far in range(HALF)]
+    sums = []
+    for d in range(depth_count):
+        up = upper(d)
+        sums.append((*pieces[d], swap(up, 2)))
+
+    def z_sum(depths):
+        many = [[(k[far] + g[far]) + n[far] for k, g, n in (sums[d] for d in depths)] for far in range(HALF)]
         parts = [x[0] if len(x) == 1 else jnp.stack(x) for x in many]
         return [parts[0]] + [swap(parts[far], far << 2) for far in range(1, HALF)]
 
-    early = sums_of([0])
-    middle = sums_of(list(range(1, depth_count - 1)))
-    tail = sums_of([depth_count - 1])
-    before = jnp.concatenate([sum(early[1:], early[0])[None], sum(middle[1:], middle[0])])
+    early = z_sum(list(range(depth_count - 2)))
+    middle = z_sum([depth_count - 2])
+    tail = z_sum([depth_count - 1])
+    before = jnp.concatenate([sum(early[1:], early[0]), sum(middle[1:], middle[0])[None]])
     before = finish_early(scale, before)
     return finish_last(scale, tail, before)
 

time: 165 us -> 160 us (0.970)
  waiting for transfers between devices: 49 us -> 43 us
    ppermute x43 -> x44, waiting for transfers between devices: 49 us -> 43 us  [swap(): return lax.ppermute(x, 'freq', [(i, i ^ mask) for i in range(n)])]
    ppermute x43 -> x44, starting transfers between devices: 61.9 us -> 63.2 us  [swap(): return lax.ppermute(x, 'freq', [(i, i ^ mask) for i in range(n)])]
  transfers between devices with their start and end apart: 43 -> 44, of which waited for: 11 -> 14; matrix products, arithmetic and copies ran while one was open for 1% -> 1% of each run, Pallas kernels for 28% -> 29%
where the time goes in v1:
time: 160 us
  starting transfers between devices  63.2 us (40%)
  Pallas kernels  48.6 us (30%)
  waiting for transfers between devices  43 us (27%)
  other arithmetic  2.5 us (2%)
  local copies, waits for them, and re-layouts  2.37 us (1%)
    ppermute x44, starting transfers between devices, swap(): return lax.ppermute(x, 'freq', [(i, i ^ mask) for i in range(n)])  63.2 us
    ppermute x44, waiting for transfers between devices, swap(): return lax.ppermute(x, 'freq', [(i, i ^ mask) for i in range(n)])  43 us
    pallas_call x4, Pallas kernels, first_call(): pl.pallas_call(lambda *r: first_kernel(dict(metas=metas, R=R), *r), out_s...  20 us
    pallas_call x5, Pallas kernels, second_call(): pl.pallas_call(lambda *r: second_kernel(dict(last=last, R=R, part=part),...  18.3 us
    pallas_call x2, Pallas kernels, prep_field(): pl.pallas_call(lambda *r: prep_field_kernel(p, sign, *r), out_shape=jax.S...  7.05 us
  transfers between devices with their start and end apart: 44, of which 14 were waited for; matrix products, arithmetic and copies ran while one was open for 1% of the time, Pallas kernels for 29%

profile of v1, /device:TPU:0, one launch (start us, length us, event | category | flops | bytes accessed | tf_op | source)
XLA Modules:
  0.0 160.1 jit_solution(500584804433680064)
XLA Ops:
  2.0 3.1 %collective-permute-start.21 = (f32[2,32,512]{2,1,0:T(8,128)S(1)}, f32[2,32,512]{2,1,0:T(8,128)S(1)}, u32[]{:S(2)}, u32[]{:S(2)}) collective-permute-start(f32[2,32,512]{2,1,0:T(8,128)S(1)} %get-tuple-element.40), channel_id=1, source_target_pairs={{0,4},{1,5},{2,6},{3,7},{4,0},{5,1},{6,2},{7,3},{8,12},{9,13},{10,... | collective-permute-start | bytes 393224 | tf_op jit(solution)/shard_map/ppermute | solution.py:403
  10.2 3.4 %collective-permute-start.16 = (f32[2,32,512]{2,1,0:T(8,128)S(1)}, f32[2,32,512]{2,1,0:T(8,128)S(1)}, u32[]{:S(2)}, u32[]{:S(2)}) collective-permute-start(f32[2,32,512]{2,1,0:T(8,128)S(1)} %get-tuple-element.39), channel_id=1, source_target_pairs={{0,8},{1,9},{2,10},{3,11},{4,12},{5,13},{6,14},{7,15},{8,0},{9,1},... | collective-permute-start | bytes 393224 | tf_op jit(solution)/shard_map/ppermute | solution.py:403
  13.6 4.4 %collective-permute-done.22 = f32[2,32,512]{2,1,0:T(8,128)S(1)} collective-permute-done((f32[2,32,512]{2,1,0:T(8,128)S(1)}, f32[2,32,512]{2,1,0:T(8,128)S(1)}, u32[]{:S(2)}, u32[]{:S(2)}) %collective-permute-start.22) | collective-permute-done | bytes 131104 | tf_op jit(solution)/shard_map/ppermute | solution.py:403
  18.0 2.9 %collective-permute-start.17 = (f32[2,32,512]{2,1,0:T(8,128)S(1)}, f32[2,32,512]{2,1,0:T(8,128)S(1)}, u32[]{:S(2)}, u32[]{:S(2)}) collective-permute-start(f32[2,32,512]{2,1,0:T(8,128)S(1)} %get-tuple-element.39), channel_id=1, source_target_pairs={{0,12},{1,13},{2,14},{3,15},{4,8},{5,9},{6,10},{7,11},{8,4},{9,5},... | collective-permute-start | bytes 393224 | tf_op jit(solution)/shard_map/ppermute | solution.py:403
  21.8 9.4 %collective-permute-start.9 = (f32[2,32,512]{2,1,0:T(8,128)S(1)}, f32[2,32,512]{2,1,0:T(8,128)S(1)}, u32[]{:S(2)}, u32[]{:S(2)}) collective-permute-start(f32[2,32,512]{2,1,0:T(8,128)S(1)} %get-tuple-element.38), channel_id=1, source_target_pairs={{0,4},{1,5},{2,6},{3,7},{4,0},{5,1},{6,2},{7,3},{8,12},{9,13},{10,... | collective-permute-start | bytes 393224 | tf_op jit(solution)/shard_map/ppermute | solution.py:403
  36.2 3.4 %collective-permute-start.3 = (f32[2,32,512]{2,1,0:T(8,128)S(1)}, f32[2,32,512]{2,1,0:T(8,128)S(1)}, u32[]{:S(2)}, u32[]{:S(2)}) collective-permute-start(f32[2,32,512]{2,1,0:T(8,128)S(1)} %get-tuple-element.37), channel_id=1, source_target_pairs={{0,4},{1,5},{2,6},{3,7},{4,0},{5,1},{6,2},{7,3},{8,12},{9,13},{10,... | collective-permute-start | bytes 393224 | tf_op jit(solution)/shard_map/ppermute | solution.py:403
  40.5 4.2 %collective-permute-done.10 = f32[2,32,512]{2,1,0:T(8,128)S(1)} collective-permute-done((f32[2,32,512]{2,1,0:T(8,128)S(1)}, f32[2,32,512]{2,1,0:T(8,128)S(1)}, u32[]{:S(2)}, u32[]{:S(2)}) %collective-permute-start.10) | collective-permute-done | bytes 131104 | tf_op jit(solution)/shard_map/ppermute | solution.py:403
  47.5 3.2 %collective-permute-start.5 = (f32[2,32,512]{2,1,0:T(8,128)S(1)}, f32[2,32,512]{2,1,0:T(8,128)S(1)}, u32[]{:S(2)}, u32[]{:S(2)}) collective-permute-start(f32[2,32,512]{2,1,0:T(8,128)S(1)} %get-tuple-element.37), channel_id=1, source_target_pairs={{0,12},{1,13},{2,14},{3,15},{4,8},{5,9},{6,10},{7,11},{8,4},{9,5},... | collective-permute-start | bytes 393224 | tf_op jit(solution)/shard_map/ppermute | solution.py:403
  57.0 9.6 %collective-permute-done.18.r_7_ = f32[3,2,32,512]{3,2,1,0:T(8,128)} collective-permute-done((f32[3,2,32,512]{3,2,1,0:T(8,128)}, f32[3,2,32,512]{3,2,1,0:T(8,128)}, u32[]{:S(2)}, u32[]{:S(2)}) %collective-permute-start.18) | collective-permute-done | bytes 393248 | tf_op jit(solution)/shard_map/ppermute | solution.py:403
  71.0 3.5 %prep_field.2.r_10_ = f32[2,64,8,512]{3,2,1,0:T(8,128)S(1)} custom-call(s32[3]{0:T(128)S(1)} %pad_add_fusion.r_0_, f32[1,2,512,512]{3,2,1,0:T(8,128)S(1)} %copy-done), custom_call_target="tpu_custom_call" | custom-call | tf_op jit(solution)/shard_map/prep_field/pallas_call | solution.py:146
  74.6 3.5 %prep_field.3.r_11_ = f32[2,64,8,512]{3,2,1,0:T(8,128)S(1)} custom-call(s32[3]{0:T(128)S(1)} %pad_add_fusion.r_0_, f32[1,2,512,512]{3,2,1,0:T(8,128)S(1)} %copy-done.1), custom_call_target="tpu_custom_call" | custom-call | tf_op jit(solution)/shard_map/prep_field/pallas_call | solution.py:146
  78.2 4.5 %first_half.4 = (f32[4,66,8,512]{3,2,1,0:T(8,128)S(1)}, f32[4,66,8,512]{3,2,1,0:T(8,128)S(1)}, f32[2,64,8,512]{3,2,1,0:T(8,128)S(1)}) custom-call(s32[3]{0:T(128)S(1)} %pad_add_fusion.r_0_, f32[2]{0:T(128)S(1)} %copy-done.8, f32[4,2,32,512]{3,2,1,0:T(8,128)S(1)} %get-tuple-element.36.r_2_, f32[4,2,32,512]{3,2,1,0:T(8,128)S(1)} %collective-permute-done.r_3_, ...), custom_call_target="tpu_custom_call" | custom-call | tf_op jit(solution)/shard_map/first_half/pallas_call | solution.py:367
  82.7 4.4 %shard_map.55 = (f32[8,32,512]{2,1,0:T(8,128)S(1)}, f32[8,32,512]{2,1,0:T(8,128)S(1)}, f32[2,64,8,512]{3,2,1,0:T(8,128)S(1)}, f32[2,64,8,512]{3,2,1,0:T(8,128)S(1)}) custom-call(s32[3]{0:T(128)S(1)} %pad_add_fusion.r_0_, f32[4,66,8,512]{3,2,1,0:T(8,128)S(1)} %get-tuple-element.41.r_1_, f32[4,66,8,512]{3,2,1,0:T(8,128)S(1)} %get-tuple-element.42.r_2_, ...), custom_call_target="tpu_custom_call" | custom-call | tf_op jit(solution)/shard_map/pallas_call | solution.py:390
  88.3 5.3 %first_half.5 = (f32[4,66,8,512]{3,2,1,0:T(8,128)S(1)}, f32[4,66,8,512]{3,2,1,0:T(8,128)S(1)}, f32[2,64,8,512]{3,2,1,0:T(8,128)S(1)}) custom-call(s32[3]{0:T(128)S(1)} %pad_add_fusion.r_0_, f32[2]{0:T(128)S(1)} %copy-done.8, f32[4,2,32,512]{3,2,1,0:T(8,128)S(1)} %get-tuple-element.36.r_2_, f32[4,2,32,512]{3,2,1,0:T(8,128)S(1)} %collective-permute-done.r_3_, ...), custom_call_target="tpu_custom_call" | custom-call | tf_op jit(solution)/shard_map/first_half/pallas_call | solution.py:367
  93.6 4.4 %shard_map.56 = (f32[8,32,512]{2,1,0:T(8,128)S(1)}, f32[8,32,512]{2,1,0:T(8,128)S(1)}, f32[2,64,8,512]{3,2,1,0:T(8,128)S(1)}, f32[2,64,8,512]{3,2,1,0:T(8,128)S(1)}) custom-call(s32[3]{0:T(128)S(1)} %pad_add_fusion.r_0_, f32[4,66,8,512]{3,2,1,0:T(8,128)S(1)} %get-tuple-element.46.r_1_, f32[4,66,8,512]{3,2,1,0:T(8,128)S(1)} %get-tuple-element.47.r_2_, ...), custom_call_target="tpu_custom_call" | custom-call | tf_op jit(solution)/shard_map/pallas_call | solution.py:390
  98.2 5.1 %first_half.6 = (f32[4,66,8,512]{3,2,1,0:T(8,128)S(1)}, f32[4,66,8,512]{3,2,1,0:T(8,128)S(1)}, f32[2,64,8,512]{3,2,1,0:T(8,128)S(1)}) custom-call(s32[3]{0:T(128)S(1)} %pad_add_fusion.r_0_, f32[2]{0:T(128)S(1)} %copy-done.8, f32[4,2,32,512]{3,2,1,0:T(8,128)S(1)} %get-tuple-element.36.r_2_, f32[4,2,32,512]{3,2,1,0:T(8,128)S(1)} %collective-permute-done.r_3_, ...), custom_call_target="tpu_custom_call" | custom-call | tf_op jit(solution)/shard_map/first_half/pallas_call | solution.py:367
  103.3 4.4 %shard_map.57 = (f32[8,32,512]{2,1,0:T(8,128)S(1)}, f32[8,32,512]{2,1,0:T(8,128)S(1)}, f32[2,64,8,512]{3,2,1,0:T(8,128)S(1)}, f32[2,64,8,512]{3,2,1,0:T(8,128)S(1)}) custom-call(s32[3]{0:T(128)S(1)} %pad_add_fusion.r_0_, f32[4,66,8,512]{3,2,1,0:T(8,128)S(1)} %get-tuple-element.51.r_1_, f32[4,66,8,512]{3,2,1,0:T(8,128)S(1)} %get-tuple-element.52.r_2_, ...), custom_call_target="tpu_custom_call" | custom-call | tf_op jit(solution)/shard_map/pallas_call | solution.py:390
  108.3 5.0 %first_half.7 = (f32[4,66,8,512]{3,2,1,0:T(8,128)S(1)}, f32[4,66,8,512]{3,2,1,0:T(8,128)S(1)}, f32[2,64,8,512]{3,2,1,0:T(8,128)S(1)}) custom-call(s32[3]{0:T(128)S(1)} %pad_add_fusion.r_0_, f32[2]{0:T(128)S(1)} %copy-done.8, f32[4,2,32,512]{3,2,1,0:T(8,128)S(1)} %get-tuple-element.36.r_2_, f32[4,2,32,512]{3,2,1,0:T(8,128)S(1)} %collective-permute-done.r_3_, ...), custom_call_target="tpu_custom_call" | custom-call | tf_op jit(solution)/shard_map/first_half/pallas_call | solution.py:367
  113.3 3.2 %shard_map.58 = (f32[8,32,512]{2,1,0:T(8,128)S(1)}, f32[4,66,8,512]{3,2,1,0:T(8,128)S(1)}) custom-call(s32[3]{0:T(128)S(1)} %pad_add_fusion.r_0_, f32[4,66,8,512]{3,2,1,0:T(8,128)S(1)} %get-tuple-element.56.r_1_, f32[4,66,8,512]{3,2,1,0:T(8,128)S(1)} %get-tuple-element.57.r_2_, f32[2,64,8,512]{3,2,1,0:T(8,128)S(1)} %get-tuple-element.58.r_3_), custom_call_target="tpu_custom_call" | custom-call | tf_op jit(solution)/shard_map/pallas_call | solution.py:390
  123.0 4.8 %collective-permute-done.33 = f32[4,32,512]{2,1,0:T(8,128)S(1)} collective-permute-done((f32[4,32,512]{2,1,0:T(8,128)S(1)}, f32[4,32,512]{2,1,0:T(8,128)S(1)}, u32[]{:S(2)}, u32[]{:S(2)}) %collective-permute-start.33) | collective-permute-done | bytes 262176 | tf_op jit(solution)/shard_map/ppermute | solution.py:403
  127.8 5.5 %collective-permute-done.35 = f32[4,32,512]{2,1,0:T(8,128)S(1)} collective-permute-done((f32[4,32,512]{2,1,0:T(8,128)S(1)}, f32[4,32,512]{2,1,0:T(8,128)S(1)}, u32[]{:S(2)}, u32[]{:S(2)}) %collective-permute-start.35) | collective-permute-done | bytes 262176 | tf_op jit(solution)/shard_map/ppermute | solution.py:403
  133.6 3.8 %collective-permute-start.37 = (f32[2,32,512]{2,1,0:T(8,128)S(1)}, f32[2,32,512]{2,1,0:T(8,128)S(1)}, u32[]{:S(2)}, u32[]{:S(2)}) collective-permute-start(f32[2,32,512]{2,1,0:T(8,128)S(1)} %pad_maximum_fusion.7), channel_id=1, source_target_pairs={{0,8},{1,9},{2,10},{3,11},{4,12},{5,13},{6,14},{7,15},{8,0},{9,1},... | collective-permute-start | bytes 393224 | tf_op jit(solution)/shard_map/ppermute | solution.py:403
  139.1 3.7 %collective-permute-start.42 = (f32[32,512]{1,0:T(8,128)S(1)}, f32[32,512]{1,0:T(8,128)S(1)}, u32[]{:S(2)}, u32[]{:S(2)}) collective-permute-start(f32[32,512]{1,0:T(8,128)S(1)} %get-tuple-element.77), channel_id=1, source_target_pairs={{0,8},{1,9},{2,10},{3,11},{4,12},{5,13},{6,14},{7,15},{8,0},{9,1},... | collective-permute-start | bytes 196616 | tf_op jit(solution)/shard_map/ppermute | solution.py:403
  144.1 3.2 %collective-permute-start.43 = (f32[32,512]{1,0:T(8,128)S(1)}, f32[32,512]{1,0:T(8,128)S(1)}, u32[]{:S(2)}, u32[]{:S(2)}) collective-permute-start(f32[32,512]{1,0:T(8,128)S(1)} %get-tuple-element.76), channel_id=1, source_target_pairs={{0,12},{1,13},{2,14},{3,15},{4,8},{5,9},{6,10},{7,11},{8,4},{9,5},... | collective-permute-start | bytes 196616 | tf_op jit(solution)/shard_map/ppermute | solution.py:403
  (116 shorter events, 51.5 us)
Async XLA Ops:
  5.1 12.9 %collective-permute-start.22 = (f32[2,32,512]{2,1,0:T(8,128)S(1)}, f32[2,32,512]{2,1,0:T(8,128)S(1)}, u32[]{:S(2)}, u32[]{:S(2)}) collective-permute-start(f32[2,32,512]{2,1,0:T(8,128)S(1)} %get-tuple-element.40), channel_id=1, source_target_pairs={{0,8},{1,9},{2,10},{3,11},{4,12},{5,13},{6,14},{7,15},{8,0},{9,1},... | collective-permute-start | bytes 393224 | tf_op jit(solution)/shard_map/ppermute | solution.py:403
  7.7 13.2 %collective-permute-start.23 = (f32[2,32,512]{2,1,0:T(8,128)S(1)}, f32[2,32,512]{2,1,0:T(8,128)S(1)}, u32[]{:S(2)}, u32[]{:S(2)}) collective-permute-start(f32[2,32,512]{2,1,0:T(8,128)S(1)} %get-tuple-element.40), channel_id=1, source_target_pairs={{0,12},{1,13},{2,14},{3,15},{4,8},{5,9},{6,10},{7,11},{8,4},{9,5},... | collective-permute-start | bytes 393224 | tf_op jit(solution)/shard_map/ppermute | solution.py:403
  7.7 43.0 %collective-permute-start = (f32[4,2,32,512]{3,2,1,0:T(8,128)S(1)}, f32[4,2,32,512]{3,2,1,0:T(8,128)S(1)}, u32[]{:S(2)}, u32[]{:S(2)}) collective-permute-start(f32[4,2,32,512]{3,2,1,0:T(8,128)S(1)} %get-tuple-element.36.r_2_), channel_id=1, source_target_pairs={{0,2},{1,3},{2,0},{3,1},{4,6},{5,7},{6,4},{7,5},{8,10},{9,11},{10,... | collective-permute-start | bytes 1572872 | tf_op jit(solution)/shard_map/ppermute | solution.py:403
  10.2 21.9 %collective-permute-start.16 = (f32[2,32,512]{2,1,0:T(8,128)S(1)}, f32[2,32,512]{2,1,0:T(8,128)S(1)}, u32[]{:S(2)}, u32[]{:S(2)}) collective-permute-start(f32[2,32,512]{2,1,0:T(8,128)S(1)} %get-tuple-element.39), channel_id=1, source_target_pairs={{0,8},{1,9},{2,10},{3,11},{4,12},{5,13},{6,14},{7,15},{8,0},{9,1},... | collective-permute-start | bytes 393224 | tf_op jit(solution)/shard_map/ppermute | solution.py:403
  18.0 15.6 %collective-permute-start.17 = (f32[2,32,512]{2,1,0:T(8,128)S(1)}, f32[2,32,512]{2,1,0:T(8,128)S(1)}, u32[]{:S(2)}, u32[]{:S(2)}) collective-permute-start(f32[2,32,512]{2,1,0:T(8,128)S(1)} %get-tuple-element.39), channel_id=1, source_target_pairs={{0,12},{1,13},{2,14},{3,15},{4,8},{5,9},{6,10},{7,11},{8,4},{9,5},... | collective-permute-start | bytes 393224 | tf_op jit(solution)/shard_map/ppermute | solution.py:403
  20.9 15.3 %collective-permute-start.11 = (f32[2,32,512]{2,1,0:T(8,128)S(1)}, f32[2,32,512]{2,1,0:T(8,128)S(1)}, u32[]{:S(2)}, u32[]{:S(2)}) collective-permute-start(f32[2,32,512]{2,1,0:T(8,128)S(1)} %get-tuple-element.38), channel_id=1, source_target_pairs={{0,12},{1,13},{2,14},{3,15},{4,8},{5,9},{6,10},{7,11},{8,4},{9,5},... | collective-permute-start | bytes 393224 | tf_op jit(solution)/shard_map/ppermute | solution.py:403
  21.8 17.8 %collective-permute-start.9 = (f32[2,32,512]{2,1,0:T(8,128)S(1)}, f32[2,32,512]{2,1,0:T(8,128)S(1)}, u32[]{:S(2)}, u32[]{:S(2)}) collective-permute-start(f32[2,32,512]{2,1,0:T(8,128)S(1)} %get-tuple-element.38), channel_id=1, source_target_pairs={{0,4},{1,5},{2,6},{3,7},{4,0},{5,1},{6,2},{7,3},{8,12},{9,13},{10,... | collective-permute-start | bytes 393224 | tf_op jit(solution)/shard_map/ppermute | solution.py:403
  32.0 23.8 %collective-permute-start.24 = (f32[3,2,32,512]{3,2,1,0:T(8,128)S(1)}, f32[3,2,32,512]{3,2,1,0:T(8,128)S(1)}, u32[]{:S(2)}, u32[]{:S(2)}) collective-permute-start(f32[3,2,32,512]{3,2,1,0:T(8,128)S(1)} %pad_maximum_fusion.4.r_6_), channel_id=1, source_target_pairs={{0,2},{1,3},{2,0},{3,1},{4,6},{5,7},{6,4},{7,5},{8,10},{9,11},{10,... | collective-permute-start | bytes 1179656 | tf_op jit(solution)/shard_map/ppermute | solution.py:403
  50.7 18.1 %collective-permute-start.2 = (f32[4,2,32,512]{3,2,1,0:T(8,128)S(1)}, f32[4,2,32,512]{3,2,1,0:T(8,128)S(1)}, u32[]{:S(2)}, u32[]{:S(2)}) collective-permute-start(f32[4,2,32,512]{3,2,1,0:T(8,128)S(1)} %collective-permute-done.r_3_), channel_id=1, source_target_pairs={{0,1},{1,0},{2,3},{3,2},{4,5},{5,4},{6,7},{7,6},{8,9},{9,8},{10,11... | collective-permute-start | bytes 1572872 | tf_op jit(solution)/shard_map/ppermute | solution.py:403
  55.8 31.3 %collective-permute-start.19 = (f32[3,2,32,512]{3,2,1,0:T(8,128)}, f32[3,2,32,512]{3,2,1,0:T(8,128)}, u32[]{:S(2)}, u32[]{:S(2)}) collective-permute-start(f32[3,2,32,512]{3,2,1,0:T(8,128)} %pad_maximum_fusion.3.r_6_), channel_id=1, source_target_pairs={{0,1},{1,0},{2,3},{3,2},{4,5},{5,4},{6,7},{7,6},{8,9},{9,8},{10,11... | collective-permute-start | bytes 1179656 | tf_op jit(solution)/shard_map/ppermute | solution.py:403
  56.4 30.9 %collective-permute-start.12 = (f32[3,2,32,512]{3,2,1,0:T(8,128)S(1)}, f32[3,2,32,512]{3,2,1,0:T(8,128)}, u32[]{:S(2)}, u32[]{:S(2)}) collective-permute-start(f32[3,2,32,512]{3,2,1,0:T(8,128)S(1)} %pad_maximum_fusion.2.r_6_), channel_id=1, source_target_pairs={{0,2},{1,3},{2,0},{3,1},{4,6},{5,7},{6,4},{7,5},{8,10},{9,11},{10,... | collective-permute-start | bytes 1179656 | tf_op jit(solution)/shard_map/ppermute | solution.py:403
  66.6 21.2 %collective-permute-start.6 = (f32[3,2,32,512]{3,2,1,0:T(8,128)S(1)}, f32[3,2,32,512]{3,2,1,0:T(8,128)}, u32[]{:S(2)}, u32[]{:S(2)}) collective-permute-start(f32[3,2,32,512]{3,2,1,0:T(8,128)S(1)} %pad_maximum_fusion.1.r_6_), channel_id=1, source_target_pairs={{0,2},{1,3},{2,0},{3,1},{4,6},{5,7},{6,4},{7,5},{8,10},{9,11},{10,... | collective-permute-start | bytes 1179656 | tf_op jit(solution)/shard_map/ppermute | solution.py:403
  68.8 19.0 %collective-permute-start.20 = (f32[3,2,32,512]{3,2,1,0:T(8,128)}, f32[3,2,32,512]{3,2,1,0:T(8,128)}, u32[]{:S(2)}, u32[]{:S(2)}) collective-permute-start(f32[3,2,32,512]{3,2,1,0:T(8,128)} %collective-permute-done.18.r_7_), channel_id=1, source_target_pairs={{0,1},{1,0},{2,3},{3,2},{4,5},{5,4},{6,7},{7,6},{8,9},{9,8},{10,11... | collective-permute-start | bytes 1179656 | tf_op jit(solution)/shard_map/ppermute | solution.py:403
  68.9 29.2 %collective-permute-start.13 = (f32[3,2,32,512]{3,2,1,0:T(8,128)S(1)}, f32[3,2,32,512]{3,2,1,0:T(8,128)}, u32[]{:S(2)}, u32[]{:S(2)}) collective-permute-start(f32[3,2,32,512]{3,2,1,0:T(8,128)S(1)} %pad_maximum_fusion.2.r_6_), channel_id=1, source_target_pairs={{0,1},{1,0},{2,3},{3,2},{4,5},{5,4},{6,7},{7,6},{8,9},{9,8},{10,11... | collective-permute-start | bytes 1179656 | tf_op jit(solution)/shard_map/ppermute | solution.py:403
  87.2 31.3 %collective-permute-start.32 = (f32[8,32,512]{2,1,0:T(8,128)S(1)}, f32[8,32,512]{2,1,0:T(8,128)S(1)}, u32[]{:S(2)}, u32[]{:S(2)}) collective-permute-start(f32[8,32,512]{2,1,0:T(8,128)S(1)} %get-tuple-element.62), channel_id=1, source_target_pairs={{0,1},{1,0},{2,3},{3,2},{4,5},{5,4},{6,7},{7,6},{8,9},{9,8},{10,11... | collective-permute-start | bytes 1572872 | tf_op jit(solution)/shard_map/ppermute | solution.py:403
  87.7 20.5 %collective-permute-start.7 = (f32[3,2,32,512]{3,2,1,0:T(8,128)S(1)}, f32[3,2,32,512]{3,2,1,0:T(8,128)S(1)}, u32[]{:S(2)}, u32[]{:S(2)}) collective-permute-start(f32[3,2,32,512]{3,2,1,0:T(8,128)S(1)} %pad_maximum_fusion.1.r_6_), channel_id=1, source_target_pairs={{0,1},{1,0},{2,3},{3,2},{4,5},{5,4},{6,7},{7,6},{8,9},{9,8},{10,11... | collective-permute-start | bytes 1179656 | tf_op jit(solution)/shard_map/ppermute | solution.py:403
  87.8 20.4 %collective-permute-start.8 = (f32[3,2,32,512]{3,2,1,0:T(8,128)}, f32[3,2,32,512]{3,2,1,0:T(8,128)S(1)}, u32[]{:S(2)}, u32[]{:S(2)}) collective-permute-start(f32[3,2,32,512]{3,2,1,0:T(8,128)} %collective-permute-done.6.r_7_), channel_id=1, source_target_pairs={{0,1},{1,0},{2,3},{3,2},{4,5},{5,4},{6,7},{7,6},{8,9},{9,8},{10,11... | collective-permute-start | bytes 1179656 | tf_op jit(solution)/shard_map/ppermute | solution.py:403
  98.1 21.0 %collective-permute-start.34 = (f32[8,32,512]{2,1,0:T(8,128)S(1)}, f32[8,32,512]{2,1,0:T(8,128)S(1)}, u32[]{:S(2)}, u32[]{:S(2)}) collective-permute-start(f32[8,32,512]{2,1,0:T(8,128)S(1)} %get-tuple-element.64), channel_id=1, source_target_pairs={{0,1},{1,0},{2,3},{3,2},{4,5},{5,4},{6,7},{7,6},{8,9},{9,8},{10,11... | collective-permute-start | bytes 1572872 | tf_op jit(solution)/shard_map/ppermute | solution.py:403
  107.8 13.0 %collective-permute-start.39 = (f32[8,32,512]{2,1,0:T(8,128)S(1)}, f32[8,32,512]{2,1,0:T(8,128)S(1)}, u32[]{:S(2)}, u32[]{:S(2)}) collective-permute-start(f32[8,32,512]{2,1,0:T(8,128)S(1)} %get-tuple-element.66), channel_id=1, source_target_pairs={{0,1},{1,0},{2,3},{3,2},{4,5},{5,4},{6,7},{7,6},{8,9},{9,8},{10,11... | collective-permute-start | bytes 1572872 | tf_op jit(solution)/shard_map/ppermute | solution.py:403
  119.1 14.2 %collective-permute-start.35 = (f32[4,32,512]{2,1,0:T(8,128)S(1)}, f32[4,32,512]{2,1,0:T(8,128)S(1)}, u32[]{:S(2)}, u32[]{:S(2)}) collective-permute-start(f32[4,32,512]{2,1,0:T(8,128)S(1)} %slice_add_fusion.1), channel_id=1, source_target_pairs={{0,2},{1,3},{2,0},{3,1},{4,6},{5,7},{6,4},{7,5},{8,10},{9,11},{10,... | collective-permute-start | bytes 786440 | tf_op jit(solution)/shard_map/ppermute | solution.py:403
  120.8 18.2 %collective-permute-start.40 = (f32[4,32,512]{2,1,0:T(8,128)S(1)}, f32[4,32,512]{2,1,0:T(8,128)S(1)}, u32[]{:S(2)}, u32[]{:S(2)}) collective-permute-start(f32[4,32,512]{2,1,0:T(8,128)S(1)} %slice_add_fusion), channel_id=1, source_target_pairs={{0,2},{1,3},{2,0},{3,1},{4,6},{5,7},{6,4},{7,5},{8,10},{9,11},{10,... | collective-permute-start | bytes 786440 | tf_op jit(solution)/shard_map/ppermute | solution.py:403
  121.4 22.7 %collective-permute-start.28 = (f32[4,32,512]{2,1,0:T(8,128)S(1)}, f32[4,32,512]{2,1,0:T(8,128)S(1)}, u32[]{:S(2)}, u32[]{:S(2)}) collective-permute-start(f32[4,32,512]{2,1,0:T(8,128)S(1)} %slice_add_fusion.3), channel_id=1, source_target_pairs={{0,2},{1,3},{2,0},{3,1},{4,6},{5,7},{6,4},{7,5},{8,10},{9,11},{10,... | collective-permute-start | bytes 786440 | tf_op jit(solution)/shard_map/ppermute | solution.py:403
  133.5 18.4 %collective-permute-start.36 = (f32[2,32,512]{2,1,0:T(8,128)S(1)}, f32[2,32,512]{2,1,0:T(8,128)S(1)}, u32[]{:S(2)}, u32[]{:S(2)}) collective-permute-start(f32[2,32,512]{2,1,0:T(8,128)S(1)} %pad_maximum_fusion.6), channel_id=1, source_target_pairs={{0,4},{1,5},{2,6},{3,7},{4,0},{5,1},{6,2},{7,3},{8,12},{9,13},{10,... | collective-permute-start | bytes 393224 | tf_op jit(solution)/shard_map/ppermute | solution.py:403
  133.6 20.7 %collective-permute-start.37 = (f32[2,32,512]{2,1,0:T(8,128)S(1)}, f32[2,32,512]{2,1,0:T(8,128)S(1)}, u32[]{:S(2)}, u32[]{:S(2)}) collective-permute-start(f32[2,32,512]{2,1,0:T(8,128)S(1)} %pad_maximum_fusion.7), channel_id=1, source_target_pairs={{0,8},{1,9},{2,10},{3,11},{4,12},{5,13},{6,14},{7,15},{8,0},{9,1},... | collective-permute-start | bytes 393224 | tf_op jit(solution)/shard_map/ppermute | solution.py:403
  (29 other events, 215.8 us)

commit v2 on v1

--- a/solution.py
+++ b/solution.py
@@ -434,19 +434,20 @@
     def upper(d):
         return pieces[d][0][HALF:] + pieces[d][1][HALF:]
 
-    sums = []
-    for d in range(depth_count):
-        up = upper(d)
-        sums.append((*pieces[d], swap(up, 2)))
-
-    def z_sum(depths):
-        many = [[(k[far] + g[far]) + n[far] for k, g, n in (sums[d] for d in depths)] for far in range(HALF)]
+    first_ones = depth_count - 2
+    joined = jnp.stack([upper(d) for d in range(first_ones)])
+    joined = swap(joined, 2)
+    nears = [joined[d] for d in range(first_ones)] + [swap(upper(d), 2) for d in range(first_ones, depth_count)]
+    sums = [(*p, n) for p, n in zip(pieces, nears)]
+
+    def z_sum(chosen):
+        many = [[(k[far] + g[far]) + n[far] for k, g, n in chosen] for far in range(HALF)]
         parts = [x[0] if len(x) == 1 else jnp.stack(x) for x in many]
         return [parts[0]] + [swap(parts[far], far << 2) for far in range(1, HALF)]
 
-    early = z_sum(list(range(depth_count - 2)))
-    middle = z_sum([depth_count - 2])
-    tail = z_sum([depth_count - 1])
+    early = z_sum(sums[:-2])
+    middle = z_sum(sums[-2:-1])
+    tail = z_sum(sums[-1:])
     before = jnp.concatenate([sum(early[1:], early[0]), sum(middle[1:], middle[0])[None]])
     before = finish_early(scale, before)
     return finish_last(scale, tail, before)

time: 160 us -> 164 us (1.025)
  starting transfers between devices: 63.2 us -> 65.2 us
    ppermute x44 -> x43, starting transfers between devices: 63.2 us -> 65.2 us  [swap(): return lax.ppermute(x, 'freq', [(i, i ^ mask) for i in range(n)])]
    ppermute x44 -> x43, waiting for transfers between devices: 43 us -> 44.2 us  [swap(): return lax.ppermute(x, 'freq', [(i, i ^ mask) for i in range(n)])]
  transfers between devices with their start and end apart: 44 -> 43, of which waited for: 14 -> 10; matrix products, arithmetic and copies ran while one was open for 1% -> 1% of each run, Pallas kernels for 29% -> 28%
where the time goes in v2:
time: 164 us; the launch traced here: 163 us
  starting transfers between devices  65.2 us (40%)
  Pallas kernels  48.6 us (30%)
  waiting for transfers between devices  44.2 us (27%)
  other arithmetic  2.56 us (2%)
  local copies, waits for them, and re-layouts  2.37 us (1%)
    ppermute x43, starting transfers between devices, swap(): return lax.ppermute(x, 'freq', [(i, i ^ mask) for i in range(n)])  65.2 us
    ppermute x43, waiting for transfers between devices, swap(): return lax.ppermute(x, 'freq', [(i, i ^ mask) for i in range(n)])  44.2 us
    pallas_call x4, Pallas kernels, first_call(): pl.pallas_call(lambda *r: first_kernel(dict(metas=metas, R=R), *r), out_s...  20 us
    pallas_call x5, Pallas kernels, second_call(): pl.pallas_call(lambda *r: second_kernel(dict(last=last, R=R, part=part),...  18.3 us
    pallas_call x2, Pallas kernels, prep_field(): pl.pallas_call(lambda *r: prep_field_kernel(p, sign, *r), out_shape=jax.S...  7.05 us
  transfers between devices with their start and end apart: 43, of which 10 were waited for; matrix products, arithmetic and copies ran while one was open for 1% of the time, Pallas kernels for 28%

profile of v2, /device:TPU:0, one launch (start us, length us, event | category | flops | bytes accessed | tf_op | source)
XLA Modules:
  0.0 163.4 jit_solution(2512479483996408177)
XLA Ops:
  2.0 3.1 %collective-permute-start.21 = (f32[2,32,512]{2,1,0:T(8,128)S(1)}, f32[2,32,512]{2,1,0:T(8,128)S(1)}, u32[]{:S(2)}, u32[]{:S(2)}) collective-permute-start(f32[2,32,512]{2,1,0:T(8,128)S(1)} %get-tuple-element.40), channel_id=1, source_target_pairs={{0,4},{1,5},{2,6},{3,7},{4,0},{5,1},{6,2},{7,3},{8,12},{9,13},{10,... | collective-permute-start | bytes 393224 | tf_op jit(solution)/shard_map/ppermute | solution.py:403
  8.6 3.5 %collective-permute-start.16 = (f32[2,32,512]{2,1,0:T(8,128)S(1)}, f32[2,32,512]{2,1,0:T(8,128)S(1)}, u32[]{:S(2)}, u32[]{:S(2)}) collective-permute-start(f32[2,32,512]{2,1,0:T(8,128)S(1)} %get-tuple-element.39), channel_id=1, source_target_pairs={{0,8},{1,9},{2,10},{3,11},{4,12},{5,13},{6,14},{7,15},{8,0},{9,1},... | collective-permute-start | bytes 393224 | tf_op jit(solution)/shard_map/ppermute | solution.py:403
  12.1 3.3 %collective-permute-start.17 = (f32[2,32,512]{2,1,0:T(8,128)S(1)}, f32[2,32,512]{2,1,0:T(8,128)S(1)}, u32[]{:S(2)}, u32[]{:S(2)}) collective-permute-start(f32[2,32,512]{2,1,0:T(8,128)S(1)} %get-tuple-element.39), channel_id=1, source_target_pairs={{0,12},{1,13},{2,14},{3,15},{4,8},{5,9},{6,10},{7,11},{8,4},{9,5},... | collective-permute-start | bytes 393224 | tf_op jit(solution)/shard_map/ppermute | solution.py:403
  19.5 2.9 %collective-permute-start.11 = (f32[2,32,512]{2,1,0:T(8,128)S(1)}, f32[2,32,512]{2,1,0:T(8,128)S(1)}, u32[]{:S(2)}, u32[]{:S(2)}) collective-permute-start(f32[2,32,512]{2,1,0:T(8,128)S(1)} %get-tuple-element.38), channel_id=1, source_target_pairs={{0,12},{1,13},{2,14},{3,15},{4,8},{5,9},{6,10},{7,11},{8,4},{9,5},... | collective-permute-start | bytes 393224 | tf_op jit(solution)/shard_map/ppermute | solution.py:403
  22.4 8.8 %collective-permute-start.9 = (f32[2,32,512]{2,1,0:T(8,128)S(1)}, f32[2,32,512]{2,1,0:T(8,128)S(1)}, u32[]{:S(2)}, u32[]{:S(2)}) collective-permute-start(f32[2,32,512]{2,1,0:T(8,128)S(1)} %get-tuple-element.38), channel_id=1, source_target_pairs={{0,4},{1,5},{2,6},{3,7},{4,0},{5,1},{6,2},{7,3},{8,12},{9,13},{10,... | collective-permute-start | bytes 393224 | tf_op jit(solution)/shard_map/ppermute | solution.py:403
  32.0 6.2 %collective-permute-start.3 = (f32[2,32,512]{2,1,0:T(8,128)S(1)}, f32[2,32,512]{2,1,0:T(8,128)S(1)}, u32[]{:S(2)}, u32[]{:S(2)}) collective-permute-start(f32[2,32,512]{2,1,0:T(8,128)S(1)} %get-tuple-element.37), channel_id=1, source_target_pairs={{0,4},{1,5},{2,6},{3,7},{4,0},{5,1},{6,2},{7,3},{8,12},{9,13},{10,... | collective-permute-start | bytes 393224 | tf_op jit(solution)/shard_map/ppermute | solution.py:403
  39.8 3.5 %collective-permute-start.4 = (f32[2,32,512]{2,1,0:T(8,128)S(1)}, f32[2,32,512]{2,1,0:T(8,128)S(1)}, u32[]{:S(2)}, u32[]{:S(2)}) collective-permute-start(f32[2,32,512]{2,1,0:T(8,128)S(1)} %get-tuple-element.37), channel_id=1, source_target_pairs={{0,8},{1,9},{2,10},{3,11},{4,12},{5,13},{6,14},{7,15},{8,0},{9,1},... | collective-permute-start | bytes 393224 | tf_op jit(solution)/shard_map/ppermute | solution.py:403
  47.8 3.9 %collective-permute-done.4 = f32[2,32,512]{2,1,0:T(8,128)S(1)} collective-permute-done((f32[2,32,512]{2,1,0:T(8,128)S(1)}, f32[2,32,512]{2,1,0:T(8,128)S(1)}, u32[]{:S(2)}, u32[]{:S(2)}) %collective-permute-start.4) | collective-permute-done | bytes 131104 | tf_op jit(solution)/shard_map/ppermute | solution.py:403
  54.0 9.6 %collective-permute-done.18.r_7_ = f32[3,2,32,512]{3,2,1,0:T(8,128)} collective-permute-done((f32[3,2,32,512]{3,2,1,0:T(8,128)}, f32[3,2,32,512]{3,2,1,0:T(8,128)}, u32[]{:S(2)}, u32[]{:S(2)}) %collective-permute-start.18) | collective-permute-done | bytes 393248 | tf_op jit(solution)/shard_map/ppermute | solution.py:403
  68.2 3.5 %prep_field.2.r_10_ = f32[2,64,8,512]{3,2,1,0:T(8,128)S(1)} custom-call(s32[3]{0:T(128)S(1)} %pad_add_fusion.r_0_, f32[1,2,512,512]{3,2,1,0:T(8,128)S(1)} %copy-done), custom_call_target="tpu_custom_call" | custom-call | tf_op jit(solution)/shard_map/prep_field/pallas_call | solution.py:146
  71.8 3.5 %prep_field.3.r_11_ = f32[2,64,8,512]{3,2,1,0:T(8,128)S(1)} custom-call(s32[3]{0:T(128)S(1)} %pad_add_fusion.r_0_, f32[1,2,512,512]{3,2,1,0:T(8,128)S(1)} %copy-done.1), custom_call_target="tpu_custom_call" | custom-call | tf_op jit(solution)/shard_map/prep_field/pallas_call | solution.py:146
  75.4 4.5 %first_half.4 = (f32[4,66,8,512]{3,2,1,0:T(8,128)S(1)}, f32[4,66,8,512]{3,2,1,0:T(8,128)S(1)}, f32[2,64,8,512]{3,2,1,0:T(8,128)S(1)}) custom-call(s32[3]{0:T(128)S(1)} %pad_add_fusion.r_0_, f32[2]{0:T(128)S(1)} %copy-done.8, f32[4,2,32,512]{3,2,1,0:T(8,128)S(1)} %get-tuple-element.36.r_2_, f32[4,2,32,512]{3,2,1,0:T(8,128)S(1)} %collective-permute-done.r_3_, ...), custom_call_target="tpu_custom_call" | custom-call | tf_op jit(solution)/shard_map/first_half/pallas_call | solution.py:367
  79.9 4.4 %shard_map.55 = (f32[8,32,512]{2,1,0:T(8,128)S(1)}, f32[8,32,512]{2,1,0:T(8,128)S(1)}, f32[2,64,8,512]{3,2,1,0:T(8,128)S(1)}, f32[2,64,8,512]{3,2,1,0:T(8,128)S(1)}) custom-call(s32[3]{0:T(128)S(1)} %pad_add_fusion.r_0_, f32[4,66,8,512]{3,2,1,0:T(8,128)S(1)} %get-tuple-element.41.r_1_, f32[4,66,8,512]{3,2,1,0:T(8,128)S(1)} %get-tuple-element.42.r_2_, ...), custom_call_target="tpu_custom_call" | custom-call | tf_op jit(solution)/shard_map/pallas_call | solution.py:390
  84.4 5.4 %first_half.5 = (f32[4,66,8,512]{3,2,1,0:T(8,128)S(1)}, f32[4,66,8,512]{3,2,1,0:T(8,128)S(1)}, f32[2,64,8,512]{3,2,1,0:T(8,128)S(1)}) custom-call(s32[3]{0:T(128)S(1)} %pad_add_fusion.r_0_, f32[2]{0:T(128)S(1)} %copy-done.8, f32[4,2,32,512]{3,2,1,0:T(8,128)S(1)} %get-tuple-element.36.r_2_, f32[4,2,32,512]{3,2,1,0:T(8,128)S(1)} %collective-permute-done.r_3_, ...), custom_call_target="tpu_custom_call" | custom-call | tf_op jit(solution)/shard_map/first_half/pallas_call | solution.py:367
  89.7 4.4 %shard_map.56 = (f32[8,32,512]{2,1,0:T(8,128)S(1)}, f32[8,32,512]{2,1,0:T(8,128)S(1)}, f32[2,64,8,512]{3,2,1,0:T(8,128)S(1)}, f32[2,64,8,512]{3,2,1,0:T(8,128)S(1)}) custom-call(s32[3]{0:T(128)S(1)} %pad_add_fusion.r_0_, f32[4,66,8,512]{3,2,1,0:T(8,128)S(1)} %get-tuple-element.46.r_1_, f32[4,66,8,512]{3,2,1,0:T(8,128)S(1)} %get-tuple-element.47.r_2_, ...), custom_call_target="tpu_custom_call" | custom-call | tf_op jit(solution)/shard_map/pallas_call | solution.py:390
  96.8 5.1 %first_half.6 = (f32[4,66,8,512]{3,2,1,0:T(8,128)S(1)}, f32[4,66,8,512]{3,2,1,0:T(8,128)S(1)}, f32[2,64,8,512]{3,2,1,0:T(8,128)S(1)}) custom-call(s32[3]{0:T(128)S(1)} %pad_add_fusion.r_0_, f32[2]{0:T(128)S(1)} %copy-done.8, f32[4,2,32,512]{3,2,1,0:T(8,128)S(1)} %get-tuple-element.36.r_2_, f32[4,2,32,512]{3,2,1,0:T(8,128)S(1)} %collective-permute-done.r_3_, ...), custom_call_target="tpu_custom_call" | custom-call | tf_op jit(solution)/shard_map/first_half/pallas_call | solution.py:367
  101.9 4.4 %shard_map.57 = (f32[8,32,512]{2,1,0:T(8,128)S(1)}, f32[8,32,512]{2,1,0:T(8,128)S(1)}, f32[2,64,8,512]{3,2,1,0:T(8,128)S(1)}, f32[2,64,8,512]{3,2,1,0:T(8,128)S(1)}) custom-call(s32[3]{0:T(128)S(1)} %pad_add_fusion.r_0_, f32[4,66,8,512]{3,2,1,0:T(8,128)S(1)} %get-tuple-element.51.r_1_, f32[4,66,8,512]{3,2,1,0:T(8,128)S(1)} %get-tuple-element.52.r_2_, ...), custom_call_target="tpu_custom_call" | custom-call | tf_op jit(solution)/shard_map/pallas_call | solution.py:390
  106.8 5.0 %first_half.7 = (f32[4,66,8,512]{3,2,1,0:T(8,128)S(1)}, f32[4,66,8,512]{3,2,1,0:T(8,128)S(1)}, f32[2,64,8,512]{3,2,1,0:T(8,128)S(1)}) custom-call(s32[3]{0:T(128)S(1)} %pad_add_fusion.r_0_, f32[2]{0:T(128)S(1)} %copy-done.8, f32[4,2,32,512]{3,2,1,0:T(8,128)S(1)} %get-tuple-element.36.r_2_, f32[4,2,32,512]{3,2,1,0:T(8,128)S(1)} %collective-permute-done.r_3_, ...), custom_call_target="tpu_custom_call" | custom-call | tf_op jit(solution)/shard_map/first_half/pallas_call | solution.py:367
  111.8 3.2 %shard_map.58 = (f32[8,32,512]{2,1,0:T(8,128)S(1)}, f32[4,66,8,512]{3,2,1,0:T(8,128)S(1)}) custom-call(s32[3]{0:T(128)S(1)} %pad_add_fusion.r_0_, f32[4,66,8,512]{3,2,1,0:T(8,128)S(1)} %get-tuple-element.56.r_1_, f32[4,66,8,512]{3,2,1,0:T(8,128)S(1)} %get-tuple-element.57.r_2_, f32[2,64,8,512]{3,2,1,0:T(8,128)S(1)} %get-tuple-element.58.r_3_), custom_call_target="tpu_custom_call" | custom-call | tf_op jit(solution)/shard_map/pallas_call | solution.py:390
  121.0 16.7 %collective-permute-done.39 = f32[4,32,512]{2,1,0:T(8,128)S(1)} collective-permute-done((f32[4,32,512]{2,1,0:T(8,128)S(1)}, f32[4,32,512]{2,1,0:T(8,128)S(1)}, u32[]{:S(2)}, u32[]{:S(2)}) %collective-permute-start.39) | collective-permute-done | bytes 262176 | tf_op jit(solution)/shard_map/ppermute | solution.py:403
  137.8 2.8 %collective-permute-start.41 = (f32[32,512]{1,0:T(8,128)S(1)}, f32[32,512]{1,0:T(8,128)S(1)}, u32[]{:S(2)}, u32[]{:S(2)}) collective-permute-start(f32[32,512]{1,0:T(8,128)S(1)} %get-tuple-element.77), channel_id=1, source_target_pairs={{0,8},{1,9},{2,10},{3,11},{4,12},{5,13},{6,14},{7,15},{8,0},{9,1},... | collective-permute-start | bytes 196616 | tf_op jit(solution)/shard_map/ppermute | solution.py:403
  150.4 3.2 %collective-permute-done.35 = f32[2,32,512]{2,1,0:T(8,128)S(1)} collective-permute-done((f32[2,32,512]{2,1,0:T(8,128)S(1)}, f32[2,32,512]{2,1,0:T(8,128)S(1)}, u32[]{:S(2)}, u32[]{:S(2)}) %collective-permute-start.35) | collective-permute-done | bytes 131104 | tf_op jit(solution)/shard_map/ppermute | solution.py:403
  153.6 2.9 %collective-permute-start.31 = (f32[32,512]{1,0:T(8,128)S(1)}, f32[32,512]{1,0:T(8,128)S(1)}, u32[]{:S(2)}, u32[]{:S(2)}) collective-permute-start(f32[32,512]{1,0:T(8,128)S(1)} %get-tuple-element.78), channel_id=1, source_target_pairs={{0,12},{1,13},{2,14},{3,15},{4,8},{5,9},{6,10},{7,11},{8,4},{9,5},... | collective-permute-start | bytes 196616 | tf_op jit(solution)/shard_map/ppermute | solution.py:403
  156.5 4.4 %collective-permute-done.36 = f32[2,32,512]{2,1,0:T(8,128)S(1)} collective-permute-done((f32[2,32,512]{2,1,0:T(8,128)S(1)}, f32[2,32,512]{2,1,0:T(8,128)S(1)}, u32[]{:S(2)}, u32[]{:S(2)}) %collective-permute-start.36) | collective-permute-done | bytes 131104 | tf_op jit(solution)/shard_map/ppermute | solution.py:403
  (115 shorter events, 44.5 us)
Async XLA Ops:
  5.1 12.9 %collective-permute-start.22 = (f32[2,32,512]{2,1,0:T(8,128)S(1)}, f32[2,32,512]{2,1,0:T(8,128)S(1)}, u32[]{:S(2)}, u32[]{:S(2)}) collective-permute-start(f32[2,32,512]{2,1,0:T(8,128)S(1)} %get-tuple-element.40), channel_id=1, source_target_pairs={{0,8},{1,9},{2,10},{3,11},{4,12},{5,13},{6,14},{7,15},{8,0},{9,1},... | collective-permute-start | bytes 393224 | tf_op jit(solution)/shard_map/ppermute | solution.py:403
  7.7 14.7 %collective-permute-start.15 = (f32[2,32,512]{2,1,0:T(8,128)S(1)}, f32[2,32,512]{2,1,0:T(8,128)S(1)}, u32[]{:S(2)}, u32[]{:S(2)}) collective-permute-start(f32[2,32,512]{2,1,0:T(8,128)S(1)} %get-tuple-element.39), channel_id=1, source_target_pairs={{0,4},{1,5},{2,6},{3,7},{4,0},{5,1},{6,2},{7,3},{8,12},{9,13},{10,... | collective-permute-start | bytes 393224 | tf_op jit(solution)/shard_map/ppermute | solution.py:403
  8.6 23.4 %collective-permute-start.16 = (f32[2,32,512]{2,1,0:T(8,128)S(1)}, f32[2,32,512]{2,1,0:T(8,128)S(1)}, u32[]{:S(2)}, u32[]{:S(2)}) collective-permute-start(f32[2,32,512]{2,1,0:T(8,128)S(1)} %get-tuple-element.39), channel_id=1, source_target_pairs={{0,8},{1,9},{2,10},{3,11},{4,12},{5,13},{6,14},{7,15},{8,0},{9,1},... | collective-permute-start | bytes 393224 | tf_op jit(solution)/shard_map/ppermute | solution.py:403
  12.1 20.0 %collective-permute-start.17 = (f32[2,32,512]{2,1,0:T(8,128)S(1)}, f32[2,32,512]{2,1,0:T(8,128)S(1)}, u32[]{:S(2)}, u32[]{:S(2)}) collective-permute-start(f32[2,32,512]{2,1,0:T(8,128)S(1)} %get-tuple-element.39), channel_id=1, source_target_pairs={{0,12},{1,13},{2,14},{3,15},{4,8},{5,9},{6,10},{7,11},{8,4},{9,5},... | collective-permute-start | bytes 393224 | tf_op jit(solution)/shard_map/ppermute | solution.py:403
  18.0 35.3 %collective-permute-start = (f32[4,2,32,512]{3,2,1,0:T(8,128)S(1)}, f32[4,2,32,512]{3,2,1,0:T(8,128)S(1)}, u32[]{:S(2)}, u32[]{:S(2)}) collective-permute-start(f32[4,2,32,512]{3,2,1,0:T(8,128)S(1)} %get-tuple-element.36.r_2_), channel_id=1, source_target_pairs={{0,2},{1,3},{2,0},{3,1},{4,6},{5,7},{6,4},{7,5},{8,10},{9,11},{10,... | collective-permute-start | bytes 1572872 | tf_op jit(solution)/shard_map/ppermute | solution.py:403
  19.5 18.7 %collective-permute-start.11 = (f32[2,32,512]{2,1,0:T(8,128)S(1)}, f32[2,32,512]{2,1,0:T(8,128)S(1)}, u32[]{:S(2)}, u32[]{:S(2)}) collective-permute-start(f32[2,32,512]{2,1,0:T(8,128)S(1)} %get-tuple-element.38), channel_id=1, source_target_pairs={{0,12},{1,13},{2,14},{3,15},{4,8},{5,9},{6,10},{7,11},{8,4},{9,5},... | collective-permute-start | bytes 393224 | tf_op jit(solution)/shard_map/ppermute | solution.py:403
  22.4 17.4 %collective-permute-start.9 = (f32[2,32,512]{2,1,0:T(8,128)S(1)}, f32[2,32,512]{2,1,0:T(8,128)S(1)}, u32[]{:S(2)}, u32[]{:S(2)}) collective-permute-start(f32[2,32,512]{2,1,0:T(8,128)S(1)} %get-tuple-element.38), channel_id=1, source_target_pairs={{0,4},{1,5},{2,6},{3,7},{4,0},{5,1},{6,2},{7,3},{8,12},{9,13},{10,... | collective-permute-start | bytes 393224 | tf_op jit(solution)/shard_map/ppermute | solution.py:403
  32.0 15.0 %collective-permute-start.3 = (f32[2,32,512]{2,1,0:T(8,128)S(1)}, f32[2,32,512]{2,1,0:T(8,128)S(1)}, u32[]{:S(2)}, u32[]{:S(2)}) collective-permute-start(f32[2,32,512]{2,1,0:T(8,128)S(1)} %get-tuple-element.37), channel_id=1, source_target_pairs={{0,4},{1,5},{2,6},{3,7},{4,0},{5,1},{6,2},{7,3},{8,12},{9,13},{10,... | collective-permute-start | bytes 393224 | tf_op jit(solution)/shard_map/ppermute | solution.py:403
  38.2 15.2 %collective-permute-start.24 = (f32[3,2,32,512]{3,2,1,0:T(8,128)S(1)}, f32[3,2,32,512]{3,2,1,0:T(8,128)S(1)}, u32[]{:S(2)}, u32[]{:S(2)}) collective-permute-start(f32[3,2,32,512]{3,2,1,0:T(8,128)S(1)} %pad_maximum_fusion.5.r_6_), channel_id=1, source_target_pairs={{0,2},{1,3},{2,0},{3,1},{4,6},{5,7},{6,4},{7,5},{8,10},{9,11},{10,... | collective-permute-start | bytes 1179656 | tf_op jit(solution)/shard_map/ppermute | solution.py:403
  47.0 16.6 %collective-permute-start.1 = (f32[4,2,32,512]{3,2,1,0:T(8,128)S(1)}, f32[4,2,32,512]{3,2,1,0:T(8,128)S(1)}, u32[]{:S(2)}, u32[]{:S(2)}) collective-permute-start(f32[4,2,32,512]{3,2,1,0:T(8,128)S(1)} %get-tuple-element.36.r_2_), channel_id=1, source_target_pairs={{0,1},{1,0},{2,3},{3,2},{4,5},{5,4},{6,7},{7,6},{8,9},{9,8},{10,11... | collective-permute-start | bytes 1572872 | tf_op jit(solution)/shard_map/ppermute | solution.py:403
  53.3 13.3 %collective-permute-start.2 = (f32[4,2,32,512]{3,2,1,0:T(8,128)S(1)}, f32[4,2,32,512]{3,2,1,0:T(8,128)S(1)}, u32[]{:S(2)}, u32[]{:S(2)}) collective-permute-start(f32[4,2,32,512]{3,2,1,0:T(8,128)S(1)} %collective-permute-done.r_3_), channel_id=1, source_target_pairs={{0,1},{1,0},{2,3},{3,2},{4,5},{5,4},{6,7},{7,6},{8,9},{9,8},{10,11... | collective-permute-start | bytes 1572872 | tf_op jit(solution)/shard_map/ppermute | solution.py:403
  53.8 30.6 %collective-permute-start.19 = (f32[3,2,32,512]{3,2,1,0:T(8,128)}, f32[3,2,32,512]{3,2,1,0:T(8,128)}, u32[]{:S(2)}, u32[]{:S(2)}) collective-permute-start(f32[3,2,32,512]{3,2,1,0:T(8,128)} %pad_maximum_fusion.4.r_6_), channel_id=1, source_target_pairs={{0,1},{1,0},{2,3},{3,2},{4,5},{5,4},{6,7},{7,6},{8,9},{9,8},{10,11... | collective-permute-start | bytes 1179656 | tf_op jit(solution)/shard_map/ppermute | solution.py:403
  63.6 20.8 %collective-permute-start.20 = (f32[3,2,32,512]{3,2,1,0:T(8,128)}, f32[3,2,32,512]{3,2,1,0:T(8,128)}, u32[]{:S(2)}, u32[]{:S(2)}) collective-permute-start(f32[3,2,32,512]{3,2,1,0:T(8,128)} %collective-permute-done.18.r_7_), channel_id=1, source_target_pairs={{0,1},{1,0},{2,3},{3,2},{4,5},{5,4},{6,7},{7,6},{8,9},{9,8},{10,11... | collective-permute-start | bytes 1179656 | tf_op jit(solution)/shard_map/ppermute | solution.py:403
  63.7 31.1 %collective-permute-start.12 = (f32[3,2,32,512]{3,2,1,0:T(8,128)S(1)}, f32[3,2,32,512]{3,2,1,0:T(8,128)}, u32[]{:S(2)}, u32[]{:S(2)}) collective-permute-start(f32[3,2,32,512]{3,2,1,0:T(8,128)S(1)} %pad_maximum_fusion.3.r_6_), channel_id=1, source_target_pairs={{0,2},{1,3},{2,0},{3,1},{4,6},{5,7},{6,4},{7,5},{8,10},{9,11},{10,... | collective-permute-start | bytes 1179656 | tf_op jit(solution)/shard_map/ppermute | solution.py:403
  66.0 29.2 %collective-permute-start.6 = (f32[3,2,32,512]{3,2,1,0:T(8,128)S(1)}, f32[3,2,32,512]{3,2,1,0:T(8,128)}, u32[]{:S(2)}, u32[]{:S(2)}) collective-permute-start(f32[3,2,32,512]{3,2,1,0:T(8,128)S(1)} %pad_maximum_fusion.2.r_6_), channel_id=1, source_target_pairs={{0,2},{1,3},{2,0},{3,1},{4,6},{5,7},{6,4},{7,5},{8,10},{9,11},{10,... | collective-permute-start | bytes 1179656 | tf_op jit(solution)/shard_map/ppermute | solution.py:403
  66.6 28.8 %collective-permute-start.13 = (f32[3,2,32,512]{3,2,1,0:T(8,128)S(1)}, f32[3,2,32,512]{3,2,1,0:T(8,128)}, u32[]{:S(2)}, u32[]{:S(2)}) collective-permute-start(f32[3,2,32,512]{3,2,1,0:T(8,128)S(1)} %pad_maximum_fusion.3.r_6_), channel_id=1, source_target_pairs={{0,1},{1,0},{2,3},{3,2},{4,5},{5,4},{6,7},{7,6},{8,9},{9,8},{10,11... | collective-permute-start | bytes 1179656 | tf_op jit(solution)/shard_map/ppermute | solution.py:403
  94.2 22.9 %collective-permute-start.33 = (f32[8,32,512]{2,1,0:T(8,128)S(1)}, f32[8,32,512]{2,1,0:T(8,128)S(1)}, u32[]{:S(2)}, u32[]{:S(2)}) collective-permute-start(f32[8,32,512]{2,1,0:T(8,128)S(1)} %get-tuple-element.64), channel_id=1, source_target_pairs={{0,1},{1,0},{2,3},{3,2},{4,5},{5,4},{6,7},{7,6},{8,9},{9,8},{10,11... | collective-permute-start | bytes 1572872 | tf_op jit(solution)/shard_map/ppermute | solution.py:403
  95.3 21.8 %collective-permute-start.32 = (f32[8,32,512]{2,1,0:T(8,128)S(1)}, f32[8,32,512]{2,1,0:T(8,128)S(1)}, u32[]{:S(2)}, u32[]{:S(2)}) collective-permute-start(f32[8,32,512]{2,1,0:T(8,128)S(1)} %get-tuple-element.62), channel_id=1, source_target_pairs={{0,1},{1,0},{2,3},{3,2},{4,5},{5,4},{6,7},{7,6},{8,9},{9,8},{10,11... | collective-permute-start | bytes 1572872 | tf_op jit(solution)/shard_map/ppermute | solution.py:403
  117.2 25.6 %collective-permute-start.34 = (f32[2,4,32,512]{3,2,1,0:T(8,128)S(1)}, f32[2,4,32,512]{3,2,1,0:T(8,128)S(1)}, u32[]{:S(2)}, u32[]{:S(2)}) collective-permute-start(f32[2,4,32,512]{3,2,1,0:T(8,128)S(1)} %pad_maximum_fusion.1), channel_id=1, source_target_pairs={{0,2},{1,3},{2,0},{3,1},{4,6},{5,7},{6,4},{7,5},{8,10},{9,11},{10,... | collective-permute-start | bytes 1572872 | tf_op jit(solution)/shard_map/ppermute | solution.py:403
  118.8 18.9 %collective-permute-start.39 = (f32[4,32,512]{2,1,0:T(8,128)S(1)}, f32[4,32,512]{2,1,0:T(8,128)S(1)}, u32[]{:S(2)}, u32[]{:S(2)}) collective-permute-start(f32[4,32,512]{2,1,0:T(8,128)S(1)} %slice_add_fusion), channel_id=1, source_target_pairs={{0,2},{1,3},{2,0},{3,1},{4,6},{5,7},{6,4},{7,5},{8,10},{9,11},{10,... | collective-permute-start | bytes 786440 | tf_op jit(solution)/shard_map/ppermute | solution.py:403
  119.5 23.3 %collective-permute-start.28 = (f32[4,32,512]{2,1,0:T(8,128)S(1)}, f32[4,32,512]{2,1,0:T(8,128)S(1)}, u32[]{:S(2)}, u32[]{:S(2)}) collective-permute-start(f32[4,32,512]{2,1,0:T(8,128)S(1)} %slice_add_fusion.3), channel_id=1, source_target_pairs={{0,2},{1,3},{2,0},{3,1},{4,6},{5,7},{6,4},{7,5},{8,10},{9,11},{10,... | collective-permute-start | bytes 786440 | tf_op jit(solution)/shard_map/ppermute | solution.py:403
  142.8 19.3 %collective-permute-start.29 = (f32[32,512]{1,0:T(8,128)S(1)}, f32[32,512]{1,0:T(8,128)S(1)}, u32[]{:S(2)}, u32[]{:S(2)}) collective-permute-start(f32[32,512]{1,0:T(8,128)S(1)} %get-tuple-element.80), channel_id=1, source_target_pairs={{0,4},{1,5},{2,6},{3,7},{4,0},{5,1},{6,2},{7,3},{8,12},{9,13},{10,... | collective-permute-start | bytes 196616 | tf_op jit(solution)/shard_map/ppermute | solution.py:403
  142.9 19.2 %collective-permute-start.30 = (f32[32,512]{1,0:T(8,128)S(1)}, f32[32,512]{1,0:T(8,128)S(1)}, u32[]{:S(2)}, u32[]{:S(2)}) collective-permute-start(f32[32,512]{1,0:T(8,128)S(1)} %get-tuple-element.79), channel_id=1, source_target_pairs={{0,8},{1,9},{2,10},{3,11},{4,12},{5,13},{6,14},{7,15},{8,0},{9,1},... | collective-permute-start | bytes 196616 | tf_op jit(solution)/shard_map/ppermute | solution.py:403
  146.6 14.3 %collective-permute-start.36 = (f32[2,32,512]{2,1,0:T(8,128)S(1)}, f32[2,32,512]{2,1,0:T(8,128)S(1)}, u32[]{:S(2)}, u32[]{:S(2)}) collective-permute-start(f32[2,32,512]{2,1,0:T(8,128)S(1)} %pad_maximum_fusion.8), channel_id=1, source_target_pairs={{0,8},{1,9},{2,10},{3,11},{4,12},{5,13},{6,14},{7,15},{8,0},{9,1},... | collective-permute-start | bytes 393224 | tf_op jit(solution)/shard_map/ppermute | solution.py:403
  (28 other events, 217.9 us)
